TPU v7x, 128 devices: a whole 4x4x4 slice. The times are simulated.
128 devices in a mesh: row: 8 (over z_hi, x), sub: 16 (over z_lo, y, core).
Axes of the slice: x: 4, y: 4, z: 4 (z_hi: 2, z_lo: 2; z = z_hi * 2 + z_lo), core: 2. Of those that a mesh axis runs over, the one named last changes fastest.
Arguments:
- ritz_coefficients: bfloat16 [16384, 2048], P('row', 'sub'), may hold values from -6 to 6
- mode_map: int32 [128, 128], P(('row', 'sub')), may hold values from 0 to 127, each once within a row
- leaf_count: int32 [128], P(('row', 'sub')), may hold values from 24 to 48, as said below
- mode_blocks: bfloat16 [133120, 2048], P(('row', 'sub'))
Outputs:
- eigenvectors: bfloat16 [262144, 2048], P(('row', 'sub'))
Inputs may be any that keep to these rules, and one draw needn't show every extreme that they name: `mode_map`: each row is a permutation of 0 to 127. `leaf_count`: some substructure uses all 48 interior modes.
All inputs are finite; a program needn't handle non-finite values.
Results may differ from a plain program's by a relative error of at most 0.001.
Values may be sent and summed in bfloat16 or wider, within the bound.
No kernel may reach another device: no remote copies, remote signals or barrier semaphores. Data moves between devices by JAX's collectives and lax.ppermute only.
A program may use at most 64 MiB of HBM per device.

v0:
```python
import jax
import jax.numpy as jnp
from jax import lax
from jax.sharding import PartitionSpec as P

SR = 16
LEVELS = 5


def from_partner(value, axis, bit):
    return lax.ppermute(value, axis, [(i, i ^ 1 << bit) for i in range(lax.axis_size(axis))])


def join_halves(own_rows, partner, upper_half):
    return jnp.where(
        upper_half,
        jnp.concatenate((partner, own_rows), axis=1),
        jnp.concatenate((own_rows, partner), axis=1),
    )


def shards(ritz_coefficients, mode_map, leaf_count, mode_blocks):
    lanczos_rows = lax.all_to_all(ritz_coefficients, "sub", split_axis=0, concat_axis=1, tiled=True)
    kept_modes = lanczos_rows.shape[0]
    width = lanczos_rows.shape[1]
    slot_ids = lax.broadcasted_iota(jnp.int32, (kept_modes, kept_modes), 1)
    placement_table = (mode_map[0][:, None] == slot_ids).astype(jnp.bfloat16)
    coeffs = lax.dot_general(
        placement_table, lanczos_rows, (((0,), (0,)), ((), ())), preferred_element_type=jnp.float32
    ).astype(jnp.bfloat16)
    leaf_width = kept_modes - LEVELS * SR
    kept_rows = lax.broadcasted_iota(jnp.int32, (leaf_width, 1), 0) < leaf_count[0]
    leaf_rows = jnp.where(kept_rows, coeffs[:leaf_width], jnp.zeros((), jnp.bfloat16))
    shares = coeffs[leaf_width:].reshape(LEVELS, SR, width)
    finished = []
    device_index = lax.axis_index(("row", "sub"))
    pending = shares
    for bit_number in range(LEVELS):
        partner = from_partner(pending, ("row", "sub"), bit_number)
        upper_half = device_index >> bit_number & 1 == 1
        pending = join_halves(pending, partner, upper_half)
        finished.append(pending[0])
        pending = pending[1:]
    all_coeffs = jnp.concatenate([leaf_rows] + finished, axis=0)
    product = lax.dot_general(
        mode_blocks, all_coeffs, (((0,), (0,)), ((), ())), preferred_element_type=jnp.float32
    )
    return product.astype(jnp.bfloat16)


def solution(mesh):
    return jax.shard_map(
        shards,
        mesh=mesh,
        in_specs=(
            P("row", "sub"),
            P(("row", "sub"), None),
            P(("row", "sub")),
            P(("row", "sub"), None),
        ),
        out_specs=P(("row", "sub"), None),
        check_vma=False,
    )
```

profile of v0, /device:TPU:0, one launch (start us, length us, event | category | flops | bytes accessed | tf_op | source)
XLA Modules:
  0.0 134.6 jit_solution(16207758471534785654)
XLA Ops:
  0.0 16.9 %all_to_all.19 = bf16[16,128,128]{2,1,0:T(8,128)(2,1)S(1)} all-to-all(bf16[16,128,128]{2,1,0:T(8,128)(2,1)} %bitcast.36), channel_id=1, replica_groups=mesh['row'=8,'sub'=16] {'sub'}, dimensions={0} | all-to-all | bytes 1048576 | tf_op jit(solution)/shard_map/all_to_all | solution.py:23
  16.9 0.3 copy.7
  17.2 1.1 convolution_convert_fusion
  18.2 0.8 copy-done.1
  19.1 0.1 collective-permute-start
  19.2 1.6 %collective-permute-done = bf16[5,16,2048]{2,1,0:T(8,128)(2,1)S(1)} collective-permute-done((bf16[5,16,2048]{2,1,0:T(8,128)(2,1)S(1)}, bf16[5,16,2048]{2,1,0:T(8,128)(2,1)S(1)}, u32[]{:S(2)}, u32[]{:S(2)}) %collective-permute-start) | collective-permute-done | bytes 327712 | tf_op jit(solution)/shard_map/ppermute | solution.py:11
  20.8 0.1 maximum_select_fusion.4
  20.9 0.1 collective-permute-start.1
  21.0 13.9 %collective-permute-done.1 = bf16[4,32,2048]{2,1,0:T(8,128)(2,1)S(1)} collective-permute-done((bf16[4,32,2048]{2,1,0:T(8,128)(2,1)S(1)}, bf16[4,32,2048]{2,1,0:T(8,128)(2,1)S(1)}, u32[]{:S(2)}, u32[]{:S(2)}) %collective-permute-start.1) | collective-permute-done | bytes 524320 | tf_op jit(solution)/shard_map/ppermute | solution.py:11
  35.0 0.2 maximum_select_fusion.3
  35.2 0.0 copy-start
  35.3 1.0 copy-done
  36.2 0.1 slice.45
  36.3 0.6 collective-permute-start.2
  36.9 19.8 %collective-permute-done.2 = bf16[3,64,2048]{2,1,0:T(8,128)(2,1)} collective-permute-done((bf16[3,64,2048]{2,1,0:T(8,128)(2,1)S(1)}, bf16[3,64,2048]{2,1,0:T(8,128)(2,1)}, u32[]{:S(2)}, u32[]{:S(2)}) %collective-permute-start.2) | collective-permute-done | bytes 786464 | tf_op jit(solution)/shard_map/ppermute | solution.py:11
  56.7 2.0 %maximum_select_fusion.2 = bf16[3,128,2048]{2,1,0:T(8,128)(2,1)S(1)} fusion(bf16[3,64,2048]{2,1,0:T(8,128)(2,1)S(1)} %slice.45, bf16[3,64,2048]{2,1,0:T(8,128)(2,1)} %collective-permute-done.2, pred[]{:T(512)S(6)} %eq.30), kind=kLoop, calls=%fused_computation.5 | loop fusion | flops 7077888 | bytes 3145729 | tf_op jit(solution)/shard_map/jit(_where)/select_n | solution.py:15
  58.7 0.1 slice.47
  58.8 0.6 collective-permute-start.3
  60.1 1.0 fusion.4
  61.2 21.3 %collective-permute-done.3 = bf16[2,128,2048]{2,1,0:T(8,128)(2,1)} collective-permute-done((bf16[2,128,2048]{2,1,0:T(8,128)(2,1)S(1)}, bf16[2,128,2048]{2,1,0:T(8,128)(2,1)}, u32[]{:S(2)}, u32[]{:S(2)}) %collective-permute-start.3) | collective-permute-done | bytes 1048608 | tf_op jit(solution)/shard_map/ppermute | solution.py:11
  82.5 2.5 %maximum_select_fusion = bf16[2,256,2048]{2,1,0:T(8,128)(2,1)S(1)} fusion(bf16[2,128,2048]{2,1,0:T(8,128)(2,1)S(1)} %slice.47, bf16[2,128,2048]{2,1,0:T(8,128)(2,1)} %collective-permute-done.3, pred[]{:T(512)S(6)} %eq.31), kind=kLoop, calls=%fused_computation.2 | loop fusion | flops 9437184 | bytes 4194305 | tf_op jit(solution)/shard_map/jit(_where)/select_n | solution.py:15
  85.0 0.2 fusion.9
  85.3 0.0 slice-start.1
  85.3 1.6 %collective-permute-start.4 = (bf16[1,256,2048]{2,1,0:T(8,128)(2,1)S(1)}, bf16[1,256,2048]{2,1,0:T(8,128)(2,1)S(1)}, u32[]{:S(2)}, u32[]{:S(2)}) collective-permute-start(bf16[1,256,2048]{2,1,0:T(8,128)(2,1)S(1)} %get-tuple-element.5), channel_id=1, source_target_pairs={{0,16},{1,17},{2,18},{3,19},{4,20},{5,21},{6,22},{7,23},{8,24},{9,... | collective-permute-start | bytes 3145736 | tf_op jit(solution)/shard_map/ppermute | solution.py:11
  86.9 1.0 fusion.3
  87.9 0.1 fusion.1
  88.0 20.1 %collective-permute-done.4 = bf16[1,256,2048]{2,1,0:T(8,128)(2,1)S(1)} collective-permute-done((bf16[1,256,2048]{2,1,0:T(8,128)(2,1)S(1)}, bf16[1,256,2048]{2,1,0:T(8,128)(2,1)S(1)}, u32[]{:S(2)}, u32[]{:S(2)}) %collective-permute-start.4) | collective-permute-done | bytes 1048608 | tf_op jit(solution)/shard_map/ppermute | solution.py:11
  108.0 1.0 fusion
  109.0 0.0 slice-done
  109.0 0.0 slice-done.1
  109.0 13.3 %convert_bitcast_fusion = bf16[2048,2048]{0,1:T(8,128)(2,1)} fusion(bf16[1040,2048]{1,0:T(8,128)(2,1)S(1)} %fusion, bf16[1040,2048]{1,0:T(8,128)(2,1)S(1)} %bitcast.39), kind=kOutput, calls=%fused_computation | convolution fusion | flops 8728346624 | bytes 16908288 | tf_op jit(solution)/shard_map/dot_general | solution.py:45
  122.4 12.2 %copy.8 = bf16[2048,2048]{1,0:T(8,128)(2,1)} copy(bf16[2048,2048]{0,1:T(8,128)(2,1)} %convert_bitcast_fusion) | data formatting | bytes 16777216 | tf_op jit(solution)/shard_map/convert_element_type | solution.py:48
  (8 shorter events, 0.1 us)
Async XLA Ops:
  18.2 0.8 copy-start.1
  19.1 1.7 %collective-permute-start = (bf16[5,16,2048]{2,1,0:T(8,128)(2,1)S(1)}, bf16[5,16,2048]{2,1,0:T(8,128)(2,1)S(1)}, u32[]{:S(2)}, u32[]{:S(2)}) collective-permute-start(bf16[5,16,2048]{2,1,0:T(8,128)(2,1)S(1)} %bitcast.33), channel_id=1, source_target_pairs={{0,1},{1,0},{2,3},{3,2},{4,5},{5,4},{6,7},{7,6},{8,9},{9,8},{10,11... | collective-permute-start | bytes 983048 | tf_op jit(solution)/shard_map/ppermute | solution.py:11
  20.9 14.0 %collective-permute-start.1 = (bf16[4,32,2048]{2,1,0:T(8,128)(2,1)S(1)}, bf16[4,32,2048]{2,1,0:T(8,128)(2,1)S(1)}, u32[]{:S(2)}, u32[]{:S(2)}) collective-permute-start(bf16[4,32,2048]{2,1,0:T(8,128)(2,1)S(1)} %slice.43), channel_id=1, source_target_pairs={{0,2},{1,3},{2,0},{3,1},{4,6},{5,7},{6,4},{7,5},{8,10},{9,11},{10,... | collective-permute-start | bytes 1572872 | tf_op jit(solution)/shard_map/ppermute | solution.py:11
  35.2 1.0 copy-start
  36.3 20.4 %collective-permute-start.2 = (bf16[3,64,2048]{2,1,0:T(8,128)(2,1)S(1)}, bf16[3,64,2048]{2,1,0:T(8,128)(2,1)}, u32[]{:S(2)}, u32[]{:S(2)}) collective-permute-start(bf16[3,64,2048]{2,1,0:T(8,128)(2,1)S(1)} %slice.45), channel_id=1, source_target_pairs={{0,4},{1,5},{2,6},{3,7},{4,0},{5,1},{6,2},{7,3},{8,12},{9,13},{10,... | collective-permute-start | bytes 2359304 | tf_op jit(solution)/shard_map/ppermute | solution.py:11
  58.8 23.7 %collective-permute-start.3 = (bf16[2,128,2048]{2,1,0:T(8,128)(2,1)S(1)}, bf16[2,128,2048]{2,1,0:T(8,128)(2,1)}, u32[]{:S(2)}, u32[]{:S(2)}) collective-permute-start(bf16[2,128,2048]{2,1,0:T(8,128)(2,1)S(1)} %slice.47), channel_id=1, source_target_pairs={{0,8},{1,9},{2,10},{3,11},{4,12},{5,13},{6,14},{7,15},{8,0},{9,1},... | collective-permute-start | bytes 3145736 | tf_op jit(solution)/shard_map/ppermute | solution.py:11
  82.5 26.5 %slice-start = ((s8[4259840]{0:T(1024)(128)(4,1)}), s8[4194304]{0:T(1024)(128)(4,1)S(1)}, s32[]{:S(2)}) async-start(s8[4259840]{0:T(1024)(128)(4,1)} %bitcast.38), calls=%async_computation.1 | async-start | bytes 8388608
  85.3 23.7 %slice-start.1 = ((s8[4259840]{0:T(1024)(128)(4,1)}), s8[65536]{0:T(1024)(128)(4,1)S(1)}, s32[]{:S(2)}) async-start(s8[4259840]{0:T(1024)(128)(4,1)} %bitcast.38), calls=%async_computation.2 | async-start | bytes 131072
  85.3 22.7 %collective-permute-start.4 = (bf16[1,256,2048]{2,1,0:T(8,128)(2,1)S(1)}, bf16[1,256,2048]{2,1,0:T(8,128)(2,1)S(1)}, u32[]{:S(2)}, u32[]{:S(2)}) collective-permute-start(bf16[1,256,2048]{2,1,0:T(8,128)(2,1)S(1)} %get-tuple-element.5), channel_id=1, source_target_pairs={{0,16},{1,17},{2,18},{3,19},{4,20},{5,21},{6,22},{7,23},{8,24},{9,... | collective-permute-start | bytes 3145736 | tf_op jit(solution)/shard_map/ppermute | solution.py:11
where the time goes:
time: 135 us
  waiting for transfers between devices  76.7 us (57%)
  blocking collectives  16.9 us (13%)
  local copies, waits for them, and re-layouts  15.8 us (12%)
  matrix products  14.4 us (11%)
  other arithmetic  6.92 us (5%)
  starting transfers between devices  2.99 us (2%)
    ppermute x5, waiting for transfers between devices, from_partner(): lax.ppermute(value, axis, [(i, i ^ 1 << bit) for i in range(lax.axis_size...  76.7 us
    all_to_all x1, blocking collectives, shards(): lax.all_to_all(ritz_coefficients, 'sub', split_axis=0, concat_axis=1, til...  16.9 us
    dot_general x1, matrix products, shards(): lax.dot_general(mode_blocks, all_coeffs, (((0,), (0,)), ((), ())), prefer...  13.3 us
    convert_element_type x1, local copies, waits for them, and re-layouts, shards(): return product.astype(jnp.bfloat16)  12.2 us
    select_n x4, other arithmetic, join_halves(): jnp.where(upper_half, jnp.concatenate((partner, own_rows), axis=1), jnp.c...  4.9 us
    ppermute x5, starting transfers between devices, from_partner(): lax.ppermute(value, axis, [(i, i ^ 1 << bit) for i in range(lax.axis_size...  2.99 us
    unnamed x12, local copies, waits for them, and re-layouts  2.87 us
  transfers between devices with their start and end apart: 5, of which 5 were waited for; matrix products, arithmetic and copies ran while one was open for 2% of the time, Pallas kernels for 0%

commit v1 on v0

v1 whole, which is shorter than its diff:
```python
import functools

import jax
import jax.numpy as jnp
from jax import lax
from jax.experimental import pallas as pl
from jax.experimental.pallas import tpu as pltpu
from jax.sharding import PartitionSpec as P


SR = 16
LEVELS = 5
LEAF = 48
PAIR = 2 * SR
AXES = ("row", "sub")


OWN = [(0, l) for l in (1, 2, 3, 4, 5)]
FIRST = (
    [(2, l) for l in (2, 3, 4, 5)]
    + [(6, l) for l in (3, 4, 5)]
    + [(4, l) for l in (3, 4, 5)]
    + [(16, 5)]
    + [(8, l) for l in (4, 5)]
    + [(24, 5)]
)
SECOND = (
    [(10, 4), (10, 5), (26, 5)]
    + [(14, 4), (14, 5), (30, 5)]
    + [(12, 4), (12, 5)]
    + [(18, 5), (22, 5), (20, 5)]
    + [(28, 5)]
)
CHUNKS = ([None] + OWN, FIRST, SECOND)
DEPTHS = (LEAF + PAIR * len(OWN), PAIR * len(FIRST), PAIR * len(SECOND))

GRANT = 20 << 20
SMALL = 6 << 20
TILES = (2048,)
LAST_TILES = (1024, 768, 256)

VMEM = pl.BlockSpec(memory_space=pltpu.VMEM)
ANY = pl.BlockSpec(memory_space=pl.ANY)


def exchange(value, mask):
    return lax.ppermute(value, AXES, [(i, i ^ mask) for i in range(128)])


def params(limit):
    return pltpu.CompilerParams(vmem_limit_bytes=limit)


def arrange_kernel(count, mine, theirs, blocks, *refs):
    outs, pick, rows, sem = refs[:-3], refs[-3], refs[-2], refs[-1]
    device = lax.axis_index("row") * lax.axis_size("sub") + lax.axis_index("sub")
    at, waits = 0, []
    for number, chunk in enumerate(CHUNKS):
        copies = []
        for share in chunk:
            if share is None:
                depth, start = LEAF, 0
            else:
                mask, level = share
                depth = PAIR
                peer = ((device ^ mask) & ((1 << level) - 1)) >> 1
                start = pl.multiple_of(SR * ((1 << level) + 1) + peer * PAIR, SR)
            copies.append(
                pltpu.make_async_copy(
                    blocks.at[pl.ds(start, depth), :], rows.at[at : at + depth, :], sem.at[number]
                )
            )
            at += depth
        for copy in copies:
            copy.start()
        waits.append(copies)
    upper = lax.axis_index("sub") % 2 == 1
    local = lax.broadcasted_iota(jnp.int32, pick.shape[1:], 0)
    for core in range(2):
        slots = jnp.where(upper == (core == 1), mine[...], theirs[...])
        pick[core] = jnp.where(local == slots, 1.0, 0.0).astype(jnp.bfloat16)
    at = 0
    for number, copies in enumerate(waits):
        for copy in copies:
            copy.wait()
        depth = DEPTHS[number]
        value = rows[at : at + depth, :]
        if number == 0:
            row = lax.broadcasted_iota(jnp.int32, (LEAF, value.shape[1]), 0)
            leaf = jnp.where(row < count[0], value[:LEAF].astype(jnp.float32), 0.0)
            value = jnp.concatenate([leaf.astype(jnp.bfloat16), value[LEAF:]], axis=0)
        outs[number][...] = value.T
        at += depth


def arrange(leaf_count, mine, theirs, blocks):
    ndof = blocks.shape[1]
    kept = mine.shape[1]
    return pl.pallas_call(
        arrange_kernel,
        out_shape=[pltpu.VMEM((ndof, depth), jnp.bfloat16) for depth in DEPTHS]
        + [pltpu.VMEM((2, kept, kept), jnp.bfloat16)],
        in_specs=[
            pl.BlockSpec(memory_space=pltpu.SMEM),
            VMEM,
            VMEM,
            pl.BlockSpec(memory_space=pltpu.HBM),
        ],
        out_specs=[VMEM] * (len(DEPTHS) + 1),
        scratch_shapes=[
            pltpu.VMEM(blocks.shape, jnp.bfloat16),
            pltpu.SemaphoreType.DMA((len(DEPTHS),)),
        ],
        compiler_params=params(GRANT),
        cost_estimate=pl.CostEstimate(flops=0, bytes_accessed=9 << 20, transcendentals=0),
        name="arrange",
    )(leaf_count, mine, theirs, pltpu.with_memory_space_constraint(blocks, pltpu.HBM))


def place_kernel(pick, blocks, _, own, swap):
    upper = lax.axis_index("sub") % 2 == 1
    width = blocks.shape[2]
    kept = pick.shape[1]
    for part in range(blocks.shape[0]):
        columns = slice(part * width, (part + 1) * width)
        even, odd = (
            jnp.dot(
                pick[core],
                blocks[part, core * kept : (core + 1) * kept, :],
                preferred_element_type=jnp.float32,
            )
            for core in range(2)
        )
        own[:LEAF, columns] = jnp.where(upper, odd[:LEAF], even[:LEAF]).astype(jnp.bfloat16)
        swap[:LEAF, columns] = jnp.where(upper, even[:LEAF], odd[:LEAF]).astype(jnp.bfloat16)
        for level in range(LEVELS):
            source = slice(LEAF + level * SR, LEAF + (level + 1) * SR)
            target = LEAF + level * PAIR
            for value in (even, odd):
                share = value[source].astype(jnp.bfloat16)
                own[target : target + SR, columns] = share
                swap[target : target + SR, columns] = share
                target += SR


def place(pick, blocks, after):
    parts, _, width = blocks.shape
    shape = pltpu.VMEM((DEPTHS[0], parts * width), jnp.bfloat16)
    return pl.pallas_call(
        place_kernel,
        out_shape=[shape, shape],
        in_specs=[VMEM, VMEM, ANY],
        out_specs=[VMEM, VMEM],
        compiler_params=params(SMALL),
        name="place",
    )(pick, blocks, after)


def collect_kernel(parts, *refs):
    count = len(refs) - len(parts)
    for part, out in zip(parts, refs[count:]):
        at = 0
        for index, start in part:
            depth = refs[index].shape[0] - start
            out[at : at + depth, :] = refs[index][start:, :]
            at += depth


def collect(pieces, parts):
    width = pieces[0].shape[1]
    return pl.pallas_call(
        functools.partial(collect_kernel, parts),
        out_shape=[
            pltpu.VMEM((sum(pieces[i].shape[0] - s for i, s in part), width), jnp.bfloat16)
            for part in parts
        ],
        in_specs=[VMEM] * len(pieces),
        out_specs=[VMEM] * len(parts),
        compiler_params=params(SMALL),
    )(*pieces)


def spans(heights):
    at = 0
    for height in heights:
        yield slice(at, at + height)
        at += height


def product_kernel(first, modes, own, got, *refs):
    total = refs[-1]
    width = own.shape[1]
    for lane, piece in enumerate((own, got)):
        columns = slice(lane * width, (lane + 1) * width)
        for rows in spans(TILES):
            value = jnp.dot(modes[rows, :], piece[...], preferred_element_type=jnp.float32)
            if not first:
                value = value + refs[0][rows, columns]
            total[rows, columns] = value


def product(modes, own, got, total=None):
    ndof, depth = modes.shape
    width = 2 * own.shape[1]
    operands = [modes, own, got] + ([] if total is None else [total])
    return pl.pallas_call(
        functools.partial(product_kernel, total is None),
        out_shape=pltpu.VMEM((ndof, width), jnp.float32),
        in_specs=[VMEM] * len(operands),
        out_specs=VMEM,
        input_output_aliases={} if total is None else {3: 0},
        compiler_params=params(GRANT),
        cost_estimate=pl.CostEstimate(
            flops=2 * ndof * width * depth, bytes_accessed=8 << 20, transcendentals=0
        ),
    )(*operands)


def finish_kernel(lane, modes, piece, total, *refs):
    out, buf, sem = refs[-3:]
    width = piece.shape[1]
    columns = slice(lane * width, (lane + 1) * width)
    core = lax.axis_index("sub") % 2
    core = 1 - core if lane else core
    sends = []
    for number, rows in enumerate(spans(LAST_TILES)):
        value = jnp.dot(modes[rows, :], piece[...], preferred_element_type=jnp.float32)
        buf[rows, :] = (value + total[rows, columns]).astype(jnp.bfloat16)
        for part in range(width // 128):
            target = pl.multiple_of((2 * part + core) * 128, 128)
            sends.append(
                pltpu.make_async_copy(
                    buf.at[rows, part * 128 : (part + 1) * 128],
                    out.at[rows, pl.ds(target, 128)],
                    sem.at[number],
                )
            )
            sends[-1].start()
    for send in sends:
        send.wait()


def finish(lane, modes, piece, total, out=None):
    ndof, depth = modes.shape
    width = piece.shape[1]
    operands = [modes, piece, total] + ([] if out is None else [out])
    return pl.pallas_call(
        functools.partial(finish_kernel, lane),
        out_shape=jax.ShapeDtypeStruct((ndof, 2 * width), jnp.bfloat16),
        in_specs=[VMEM] * 3 + [ANY] * (len(operands) - 3),
        out_specs=ANY,
        scratch_shapes=[
            pltpu.VMEM((ndof, width), jnp.bfloat16),
            pltpu.SemaphoreType.DMA((len(LAST_TILES),)),
        ],
        input_output_aliases={} if out is None else {3: 0},
        compiler_params=params(GRANT),
        cost_estimate=pl.CostEstimate(
            flops=2 * ndof * width * depth, bytes_accessed=8 << 20, transcendentals=0
        ),
    )(*operands)


def shards(ritz_coefficients, mode_map, leaf_count, mode_blocks):
    *modes, pick = arrange(leaf_count, mode_map, exchange(mode_map, 1), mode_blocks)
    parts = lax.axis_size("sub") // 2
    width = ritz_coefficients.shape[1]
    lanes = [[2 * part + core for part in range(parts)] for core in range(2)]
    blocks = lax.all_to_all(
        ritz_coefficients.reshape(parts, -1, width),
        "sub",
        split_axis=0,
        concat_axis=0,
        tiled=True,
        axis_index_groups=lanes,
    )
    own, swap = place(pick, blocks, modes[0])

    def shares(low):
        return own[LEAF + (low - 1) * PAIR :]

    got = exchange(swap, 1)
    f = exchange(shares(2), 2)
    g = exchange(shares(3), 6)
    h = exchange(shares(3), 4)
    z = exchange(shares(4), 8)
    x = exchange(shares(5), 16)
    xz = exchange(shares(5), 24)
    total = product(modes[0], own, got)
    own, along_y, along_x = collect(
        [f, g, h, x, z, xz],
        [
            [(i, 0) for i in range(6)],
            [(4, 0), (5, 0)],
            [(0, 3 * PAIR), (1, 2 * PAIR), (2, 2 * PAIR)],
        ],
    )
    second = [
        exchange(along_y, 2),
        exchange(along_y, 6),
        exchange(h[PAIR:], 8),
        exchange(along_x, 16),
        exchange(h[2 * PAIR :], 24),
    ]
    got = exchange(own, 1)
    total = product(modes[1], own, got, total)
    (own,) = collect(second, [[(i, 0) for i in range(5)]])
    got = exchange(own, 1)
    out = finish(0, modes[2], own, total)
    return finish(1, modes[2], got, total, out)


def solution(mesh):
    return jax.shard_map(
        shards,
        mesh=mesh,
        in_specs=(
            P("row", "sub"),
            P(("row", "sub"), None),
            P(("row", "sub")),
            P(("row", "sub"), None),
        ),
        out_specs=P(("row", "sub"), None),
        check_vma=False,
    )
```

time: 135 us -> 63.7 us (0.47)
  the two profiles are of different devices: /device:TPU:0 before, /device:TPU:1 now
where the time goes in v1:
time: 63.7 us; the launch traced here: 63.5 us
  starting transfers between devices  23.5 us (37%)
  Pallas kernels  19 us (30%)
  waiting for transfers between devices  18 us (28%)
  local copies, waits for them, and re-layouts  2.04 us (3%)
  between operations  0.94 us (1%)
    ppermute x15, starting transfers between devices, exchange(): return lax.ppermute(value, AXES, [(i, i ^ mask) for i in range(128)])  17.2 us
    ppermute x15, waiting for transfers between devices, exchange(): return lax.ppermute(value, AXES, [(i, i ^ mask) for i in range(128)])  14.6 us
    pallas_call x2, Pallas kernels, product(): pl.pallas_call(functools.partial(product_kernel, total is None), out_shap...  8.91 us
    pallas_call x2, Pallas kernels, finish(): pl.pallas_call(functools.partial(finish_kernel, lane), out_shape=jax.Shap...  6.76 us
    all_to_all x1, starting transfers between devices, shards(): lax.all_to_all(ritz_coefficients.reshape(parts, -1, width), 'sub', split_...  6.36 us
    all_to_all x1, waiting for transfers between devices, shards(): lax.all_to_all(ritz_coefficients.reshape(parts, -1, width), 'sub', split_...  3.47 us
    pallas_call x1, Pallas kernels, arrange(): pl.pallas_call(arrange_kernel, out_shape=[pltpu.VMEM((ndof, depth), jnp.b...  2.88 us
    unnamed x6, local copies, waits for them, and re-layouts  1.97 us
  transfers between devices with their start and end apart: 16, of which 10 were waited for; matrix products, arithmetic and copies ran while one was open for 0% of the time, Pallas kernels for 24%

profile of v1, /device:TPU:1, one launch (start us, length us, event | category | flops | bytes accessed | tf_op | source)
XLA Modules:
  0.0 63.5 jit_solution(14774448976199427789)
XLA Ops:
  0.0 6.4 %all-to-all-start = ((bf16[8,256,128]{2,1,0:T(8,128)(2,1)}), bf16[8,256,128]{2,1,0:T(8,128)(2,1)S(1)}, u32[]{:S(2)}, u32[]{:S(2)}) async-start(bf16[8,256,128]{2,1,0:T(8,128)(2,1)} %bitcast.1), calls=%async_computation | async-start | bytes 1048576 | tf_op jit(solution)/shard_map/all_to_all | solution.py:269
  6.4 1.0 %collective-permute-start = (s32[1,128]{1,0:T(1,128)}, s32[1,128]{1,0:T(1,128)S(1)}, u32[]{:S(2)}, u32[]{:S(2)}) collective-permute-start(s32[1,128]{1,0:T(1,128)} %mine.1), channel_id=1, source_target_pairs={{0,1},{1,0},{2,3},{3,2},{4,5},{5,4},{6,7},{7,6},{8,9},{9,8},{10,11... | collective-permute-start | bytes 1544 | tf_op jit(solution)/shard_map/ppermute | solution.py:47
  8.0 0.3 collective-permute-done.theirs
  8.3 0.7 %copy-done.2 = s32[1,128]{1,0:T(1,128)S(1)} copy-done((s32[1,128]{1,0:T(1,128)S(1)}, s32[1,128]{1,0:T(1,128)}, u32[]{:S(2)}) %copy-start.2) | copy-done | bytes 536
  8.9 2.9 %arrange.1 = (bf16[2048,208]{1,0:T(8,128)(2,1)S(1)}, bf16[2048,448]{1,0:T(8,128)(2,1)S(1)}, bf16[2048,384]{1,0:T(8,128)(2,1)S(1)}, bf16[2,128,128]{2,1,0:T(8,128)(2,1)S(1)}) custom-call(s32[1]{0:T(128)S(6)} %copy.9.count, s32[1,128]{1,0:T(1,128)S(1)} %copy-done.2, s32[1,128]{1,0:T(1,128)S(1)} %collective-permute-done.theirs, bf16[1040,2048]{1,0:T(8,128)(2,1)} %blocks.1), custom_call_target="tpu_custom_call" | custom-call | bytes 9437184 | tf_op jit(solution)/shard_map/arrange/pallas_call | solution.py:99
  11.8 1.3 %copy-done = bf16[2048,448]{1,0:T(8,128)(2,1)} copy-done((bf16[2048,448]{1,0:T(8,128)(2,1)}, bf16[2048,448]{1,0:T(8,128)(2,1)S(1)}, u32[]{:S(2)}) %copy-start) | copy-done | bytes 1835032
  13.1 3.5 %all-to-all-done.blocks = bf16[8,256,128]{2,1,0:T(8,128)(2,1)S(1)} async-done(((bf16[8,256,128]{2,1,0:T(8,128)(2,1)}), bf16[8,256,128]{2,1,0:T(8,128)(2,1)S(1)}, u32[]{:S(2)}, u32[]{:S(2)}) %all-to-all-start) | async-done | bytes 524320 | tf_op jit(solution)/shard_map/all_to_all | solution.py:269
  16.6 0.3 place.1
  17.1 0.7 %collective-permute-start.3 = (bf16[96,1024]{1,0:T(8,128)(2,1)S(1)}, bf16[96,1024]{1,0:T(8,128)(2,1)S(1)}, u32[]{:S(2)}, u32[]{:S(2)}) collective-permute-start(bf16[96,1024]{1,0:T(8,128)(2,1)S(1)} %slice.21), channel_id=1, source_target_pairs={{0,4},{1,5},{2,6},{3,7},{4,0},{5,1},{6,2},{7,3},{8,12},{9,13},{10,... | collective-permute-start | bytes 589832 | tf_op jit(solution)/shard_map/ppermute | solution.py:47
  17.8 3.2 %collective-permute-start.2 = (bf16[96,1024]{1,0:T(8,128)(2,1)S(1)}, bf16[96,1024]{1,0:T(8,128)(2,1)S(1)}, u32[]{:S(2)}, u32[]{:S(2)}) collective-permute-start(bf16[96,1024]{1,0:T(8,128)(2,1)S(1)} %slice.21), channel_id=1, source_target_pairs={{0,6},{1,7},{2,4},{3,5},{4,2},{5,3},{6,0},{7,1},{8,14},{9,15},{10,... | collective-permute-start | bytes 589832 | tf_op jit(solution)/shard_map/ppermute | solution.py:47
  21.0 1.2 %collective-permute-start.4 = (bf16[32,1024]{1,0:T(8,128)(2,1)S(1)}, bf16[32,1024]{1,0:T(8,128)(2,1)S(1)}, u32[]{:S(2)}, u32[]{:S(2)}) collective-permute-start(bf16[32,1024]{1,0:T(8,128)(2,1)S(1)} %slice.22), channel_id=1, source_target_pairs={{0,16},{1,17},{2,18},{3,19},{4,20},{5,21},{6,22},{7,23},{8,24},{9,... | collective-permute-start | bytes 196616 | tf_op jit(solution)/shard_map/ppermute | solution.py:47
  22.2 0.4 collective-permute-start.5
  22.6 1.8 %collective-permute-done.4.refs_3_ = bf16[32,1024]{1,0:T(8,128)(2,1)S(1)} collective-permute-done((bf16[32,1024]{1,0:T(8,128)(2,1)S(1)}, bf16[32,1024]{1,0:T(8,128)(2,1)S(1)}, u32[]{:S(2)}, u32[]{:S(2)}) %collective-permute-start.4) | collective-permute-done | bytes 65568 | tf_op jit(solution)/shard_map/ppermute | solution.py:47
  24.4 1.2 %collective-permute-start.6 = (bf16[32,1024]{1,0:T(8,128)(2,1)S(1)}, bf16[32,1024]{1,0:T(8,128)(2,1)S(1)}, u32[]{:S(2)}, u32[]{:S(2)}) collective-permute-start(bf16[32,1024]{1,0:T(8,128)(2,1)S(1)} %slice.22), channel_id=1, source_target_pairs={{0,24},{1,25},{2,26},{3,27},{4,28},{5,29},{6,30},{7,31},{8,16},{9,... | collective-permute-start | bytes 196616 | tf_op jit(solution)/shard_map/ppermute | solution.py:47
  25.6 3.1 %collective-permute-done.6.refs_5_ = bf16[32,1024]{1,0:T(8,128)(2,1)S(1)} collective-permute-done((bf16[32,1024]{1,0:T(8,128)(2,1)S(1)}, bf16[32,1024]{1,0:T(8,128)(2,1)S(1)}, u32[]{:S(2)}, u32[]{:S(2)}) %collective-permute-start.6) | collective-permute-done | bytes 65568 | tf_op jit(solution)/shard_map/ppermute | solution.py:47
  28.7 0.7 %collective-permute-done.2.refs_1_ = bf16[96,1024]{1,0:T(8,128)(2,1)S(1)} collective-permute-done((bf16[96,1024]{1,0:T(8,128)(2,1)S(1)}, bf16[96,1024]{1,0:T(8,128)(2,1)S(1)}, u32[]{:S(2)}, u32[]{:S(2)}) %collective-permute-start.2) | collective-permute-done | bytes 196640 | tf_op jit(solution)/shard_map/ppermute | solution.py:47
  29.5 2.7 %collective-permute-start.13 = (bf16[448,1024]{1,0:T(8,128)(2,1)S(1)}, bf16[448,1024]{1,0:T(8,128)(2,1)S(1)}, u32[]{:S(2)}, u32[]{:S(2)}) collective-permute-start(bf16[448,1024]{1,0:T(8,128)(2,1)S(1)} %get-tuple-element.21.own), channel_id=1, source_target_pairs={{0,1},{1,0},{2,3},{3,2},{4,5},{5,4},{6,7},{7,6},{8,9},{9,8},{10,11... | collective-permute-start | bytes 2752520 | tf_op jit(solution)/shard_map/ppermute | solution.py:47
  32.3 0.4 collective-permute-start.9
  32.6 0.3 collective-permute-start.14
  32.9 2.1 %collective-permute-start.11 = (bf16[32,1024]{1,0:T(8,128)(2,1)S(1)}, bf16[32,1024]{1,0:T(8,128)(2,1)S(1)}, u32[]{:S(2)}, u32[]{:S(2)}) collective-permute-start(bf16[32,1024]{1,0:T(8,128)(2,1)S(1)} %slice.27), channel_id=1, source_target_pairs={{0,24},{1,25},{2,26},{3,27},{4,28},{5,29},{6,30},{7,31},{8,16},{9,... | collective-permute-start | bytes 196616 | tf_op jit(solution)/shard_map/ppermute | solution.py:47
  35.0 0.3 collective-permute-start.10
  35.3 2.0 %collective-permute-done.11.refs_4_ = bf16[32,1024]{1,0:T(8,128)(2,1)S(1)} collective-permute-done((bf16[32,1024]{1,0:T(8,128)(2,1)S(1)}, bf16[32,1024]{1,0:T(8,128)(2,1)S(1)}, u32[]{:S(2)}, u32[]{:S(2)}) %collective-permute-start.11) | collective-permute-done | bytes 65568 | tf_op jit(solution)/shard_map/ppermute | solution.py:47
  37.3 1.5 %collective-permute-done.9.refs_2_ = bf16[64,1024]{1,0:T(8,128)(2,1)S(1)} collective-permute-done((bf16[64,1024]{1,0:T(8,128)(2,1)S(1)}, bf16[64,1024]{1,0:T(8,128)(2,1)S(1)}, u32[]{:S(2)}, u32[]{:S(2)}) %collective-permute-start.9) | collective-permute-done | bytes 131104 | tf_op jit(solution)/shard_map/ppermute | solution.py:47
  38.8 1.6 %collective-permute-start.8 = (bf16[96,1024]{1,0:T(8,128)(2,1)S(1)}, bf16[96,1024]{1,0:T(8,128)(2,1)S(1)}, u32[]{:S(2)}, u32[]{:S(2)}) collective-permute-start(bf16[96,1024]{1,0:T(8,128)(2,1)S(1)} %get-tuple-element.18), channel_id=1, source_target_pairs={{0,6},{1,7},{2,4},{3,5},{4,2},{5,3},{6,0},{7,1},{8,14},{9,15},{10,... | collective-permute-start | bytes 589832 | tf_op jit(solution)/shard_map/ppermute | solution.py:47
  40.4 1.1 %collective-permute-done.10.refs_3_ = bf16[96,1024]{1,0:T(8,128)(2,1)S(1)} collective-permute-done((bf16[96,1024]{1,0:T(8,128)(2,1)S(1)}, bf16[96,1024]{1,0:T(8,128)(2,1)S(1)}, u32[]{:S(2)}, u32[]{:S(2)}) %collective-permute-start.10) | collective-permute-done | bytes 196640 | tf_op jit(solution)/shard_map/ppermute | solution.py:47
  41.5 0.9 %collective-permute-done.7.refs_0_ = bf16[96,1024]{1,0:T(8,128)(2,1)S(1)} collective-permute-done((bf16[96,1024]{1,0:T(8,128)(2,1)S(1)}, bf16[96,1024]{1,0:T(8,128)(2,1)S(1)}, u32[]{:S(2)}, u32[]{:S(2)}) %collective-permute-start.7) | collective-permute-done | bytes 196640 | tf_op jit(solution)/shard_map/ppermute | solution.py:47
  42.4 3.2 %collective-permute-done.8.refs_1_ = bf16[96,1024]{1,0:T(8,128)(2,1)S(1)} collective-permute-done((bf16[96,1024]{1,0:T(8,128)(2,1)S(1)}, bf16[96,1024]{1,0:T(8,128)(2,1)S(1)}, u32[]{:S(2)}, u32[]{:S(2)}) %collective-permute-start.8) | collective-permute-done | bytes 196640 | tf_op jit(solution)/shard_map/ppermute | solution.py:47
  45.6 2.0 %collective-permute-start.12 = (bf16[384,1024]{1,0:T(8,128)(2,1)S(1)}, bf16[384,1024]{1,0:T(8,128)(2,1)S(1)}, u32[]{:S(2)}, u32[]{:S(2)}) collective-permute-start(bf16[384,1024]{1,0:T(8,128)(2,1)S(1)} %shard_map.47.piece), channel_id=1, source_target_pairs={{0,1},{1,0},{2,3},{3,2},{4,5},{5,4},{6,7},{7,6},{8,9},{9,8},{10,11... | collective-permute-start | bytes 2359304 | tf_op jit(solution)/shard_map/ppermute | solution.py:47
  47.6 2.3 %shard_map.48.refs_0_ = f32[2048,2048]{1,0:T(8,128)S(1)} custom-call(bf16[2048,208]{1,0:T(8,128)(2,1)S(1)} %get-tuple-element.16._.modes, bf16[208,1024]{1,0:T(8,128)(2,1)S(1)} %get-tuple-element.17.own, bf16[208,1024]{1,0:T(8,128)(2,1)S(1)} %collective-permute-done.14.got), custom_call_target="tpu_custom_call" | custom-call | flops 1744830464 | bytes 8388608 | tf_op jit(solution)/shard_map/pallas_call | solution.py:206
  50.0 6.6 %shard_map.49.total = f32[2048,2048]{1,0:T(8,128)S(1)} custom-call(bf16[2048,448]{1,0:T(8,128)(2,1)S(1)} %copy-done.1, bf16[448,1024]{1,0:T(8,128)(2,1)S(1)} %get-tuple-element.21.own, bf16[448,1024]{1,0:T(8,128)(2,1)S(1)} %collective-permute-done.13.got, f32[2048,2048]{1,0:T(8,128)S(1)} %shard_map.48.refs_0_), custom_call_target="tpu_custom_call", output_to_operand_aliasing={{}: (3, {})} | custom-call | flops 3758096384 | bytes 8388608 | tf_op jit(solution)/shard_map/pallas_call | solution.py:206
  56.6 3.4 %shard_map.50.refs_0_ = bf16[2048,2048]{1,0:T(8,128)(2,1)} custom-call(bf16[2048,384]{1,0:T(8,128)(2,1)S(1)} %get-tuple-element.14.modes, bf16[384,1024]{1,0:T(8,128)(2,1)S(1)} %shard_map.47.piece, f32[2048,2048]{1,0:T(8,128)S(1)} %shard_map.49.total), custom_call_target="tpu_custom_call" | custom-call | flops 1610612736 | bytes 8388608 | tf_op jit(solution)/shard_map/pallas_call | solution.py:247
  60.0 3.4 %shard_map.51 = bf16[2048,2048]{1,0:T(8,128)(2,1)} custom-call(bf16[2048,384]{1,0:T(8,128)(2,1)S(1)} %get-tuple-element.14.modes, bf16[384,1024]{1,0:T(8,128)(2,1)S(1)} %collective-permute-done.12.piece, f32[2048,2048]{1,0:T(8,128)S(1)} %shard_map.49.total, bf16[2048,2048]{1,0:T(8,128)(2,1)} %shard_map.50.refs_0_), custom_call_target="tpu_custom_call", output_to_operand_aliasing={{}: (3, {})} | custom-call | flops 1610612736 | bytes 8388608 | tf_op jit(solution)/shard_map/pallas_call | solution.py:247
  (20 shorter events, 0.3 us)
Async XLA Ops:
  0.0 16.6 %all-to-all-start = ((bf16[8,256,128]{2,1,0:T(8,128)(2,1)}), bf16[8,256,128]{2,1,0:T(8,128)(2,1)S(1)}, u32[]{:S(2)}, u32[]{:S(2)}) async-start(bf16[8,256,128]{2,1,0:T(8,128)(2,1)} %bitcast.1), calls=%async_computation | async-start | bytes 1048576 | tf_op jit(solution)/shard_map/all_to_all | solution.py:269
  6.4 1.9 %collective-permute-start = (s32[1,128]{1,0:T(1,128)}, s32[1,128]{1,0:T(1,128)S(1)}, u32[]{:S(2)}, u32[]{:S(2)}) collective-permute-start(s32[1,128]{1,0:T(1,128)} %mine.1), channel_id=1, source_target_pairs={{0,1},{1,0},{2,3},{3,2},{4,5},{5,4},{6,7},{7,6},{8,9},{9,8},{10,11... | collective-permute-start | bytes 1544 | tf_op jit(solution)/shard_map/ppermute | solution.py:47
  8.3 0.7 %copy-start.2 = (s32[1,128]{1,0:T(1,128)S(1)}, s32[1,128]{1,0:T(1,128)}, u32[]{:S(2)}) copy-start(s32[1,128]{1,0:T(1,128)} %mine.1) | copy-start | bytes 1540
  11.8 1.3 %copy-start = (bf16[2048,448]{1,0:T(8,128)(2,1)}, bf16[2048,448]{1,0:T(8,128)(2,1)S(1)}, u32[]{:S(2)}) copy-start(bf16[2048,448]{1,0:T(8,128)(2,1)S(1)} %get-tuple-element.20.modes) | copy-start | bytes 5505028
  16.9 12.5 %collective-permute-start.1 = (bf16[128,1024]{1,0:T(8,128)(2,1)S(1)}, bf16[128,1024]{1,0:T(8,128)(2,1)S(1)}, u32[]{:S(2)}, u32[]{:S(2)}) collective-permute-start(bf16[128,1024]{1,0:T(8,128)(2,1)S(1)} %slice.20), channel_id=1, source_target_pairs={{0,2},{1,3},{2,0},{3,1},{4,6},{5,7},{6,4},{7,5},{8,10},{9,11},{10,... | collective-permute-start | bytes 786440 | tf_op jit(solution)/shard_map/ppermute | solution.py:47
  17.1 11.7 %collective-permute-start.3 = (bf16[96,1024]{1,0:T(8,128)(2,1)S(1)}, bf16[96,1024]{1,0:T(8,128)(2,1)S(1)}, u32[]{:S(2)}, u32[]{:S(2)}) collective-permute-start(bf16[96,1024]{1,0:T(8,128)(2,1)S(1)} %slice.21), channel_id=1, source_target_pairs={{0,4},{1,5},{2,6},{3,7},{4,0},{5,1},{6,2},{7,3},{8,12},{9,13},{10,... | collective-permute-start | bytes 589832 | tf_op jit(solution)/shard_map/ppermute | solution.py:47
  17.8 11.6 %collective-permute-start.2 = (bf16[96,1024]{1,0:T(8,128)(2,1)S(1)}, bf16[96,1024]{1,0:T(8,128)(2,1)S(1)}, u32[]{:S(2)}, u32[]{:S(2)}) collective-permute-start(bf16[96,1024]{1,0:T(8,128)(2,1)S(1)} %slice.21), channel_id=1, source_target_pairs={{0,6},{1,7},{2,4},{3,5},{4,2},{5,3},{6,0},{7,1},{8,14},{9,15},{10,... | collective-permute-start | bytes 589832 | tf_op jit(solution)/shard_map/ppermute | solution.py:47
  21.0 3.4 %collective-permute-start.4 = (bf16[32,1024]{1,0:T(8,128)(2,1)S(1)}, bf16[32,1024]{1,0:T(8,128)(2,1)S(1)}, u32[]{:S(2)}, u32[]{:S(2)}) collective-permute-start(bf16[32,1024]{1,0:T(8,128)(2,1)S(1)} %slice.22), channel_id=1, source_target_pairs={{0,16},{1,17},{2,18},{3,19},{4,20},{5,21},{6,22},{7,23},{8,24},{9,... | collective-permute-start | bytes 196616 | tf_op jit(solution)/shard_map/ppermute | solution.py:47
  22.2 6.5 %collective-permute-start.5 = (bf16[64,1024]{1,0:T(8,128)(2,1)S(1)}, bf16[64,1024]{1,0:T(8,128)(2,1)S(1)}, u32[]{:S(2)}, u32[]{:S(2)}) collective-permute-start(bf16[64,1024]{1,0:T(8,128)(2,1)S(1)} %slice.23), channel_id=1, source_target_pairs={{0,8},{1,9},{2,10},{3,11},{4,12},{5,13},{6,14},{7,15},{8,0},{9,1},... | collective-permute-start | bytes 393224 | tf_op jit(solution)/shard_map/ppermute | solution.py:47
  24.4 4.3 %collective-permute-start.6 = (bf16[32,1024]{1,0:T(8,128)(2,1)S(1)}, bf16[32,1024]{1,0:T(8,128)(2,1)S(1)}, u32[]{:S(2)}, u32[]{:S(2)}) collective-permute-start(bf16[32,1024]{1,0:T(8,128)(2,1)S(1)} %slice.22), channel_id=1, source_target_pairs={{0,24},{1,25},{2,26},{3,27},{4,28},{5,29},{6,30},{7,31},{8,16},{9,... | collective-permute-start | bytes 196616 | tf_op jit(solution)/shard_map/ppermute | solution.py:47
  29.5 20.5 %collective-permute-start.13 = (bf16[448,1024]{1,0:T(8,128)(2,1)S(1)}, bf16[448,1024]{1,0:T(8,128)(2,1)S(1)}, u32[]{:S(2)}, u32[]{:S(2)}) collective-permute-start(bf16[448,1024]{1,0:T(8,128)(2,1)S(1)} %get-tuple-element.21.own), channel_id=1, source_target_pairs={{0,1},{1,0},{2,3},{3,2},{4,5},{5,4},{6,7},{7,6},{8,9},{9,8},{10,11... | collective-permute-start | bytes 2752520 | tf_op jit(solution)/shard_map/ppermute | solution.py:47
  32.3 6.5 %collective-permute-start.9 = (bf16[64,1024]{1,0:T(8,128)(2,1)S(1)}, bf16[64,1024]{1,0:T(8,128)(2,1)S(1)}, u32[]{:S(2)}, u32[]{:S(2)}) collective-permute-start(bf16[64,1024]{1,0:T(8,128)(2,1)S(1)} %slice.26), channel_id=1, source_target_pairs={{0,8},{1,9},{2,10},{3,11},{4,12},{5,13},{6,14},{7,15},{8,0},{9,1},... | collective-permute-start | bytes 393224 | tf_op jit(solution)/shard_map/ppermute | solution.py:47
  32.6 15.0 %collective-permute-start.14 = (bf16[208,1024]{1,0:T(8,128)(2,1)S(1)}, bf16[208,1024]{1,0:T(8,128)(2,1)S(1)}, u32[]{:S(2)}, u32[]{:S(2)}) collective-permute-start(bf16[208,1024]{1,0:T(8,128)(2,1)S(1)} %get-tuple-element.22), channel_id=1, source_target_pairs={{0,1},{1,0},{2,3},{3,2},{4,5},{5,4},{6,7},{7,6},{8,9},{9,8},{10,11... | collective-permute-start | bytes 1277960 | tf_op jit(solution)/shard_map/ppermute | solution.py:47
  32.9 4.3 %collective-permute-start.11 = (bf16[32,1024]{1,0:T(8,128)(2,1)S(1)}, bf16[32,1024]{1,0:T(8,128)(2,1)S(1)}, u32[]{:S(2)}, u32[]{:S(2)}) collective-permute-start(bf16[32,1024]{1,0:T(8,128)(2,1)S(1)} %slice.27), channel_id=1, source_target_pairs={{0,24},{1,25},{2,26},{3,27},{4,28},{5,29},{6,30},{7,31},{8,16},{9,... | collective-permute-start | bytes 196616 | tf_op jit(solution)/shard_map/ppermute | solution.py:47
  35.0 6.4 %collective-permute-start.10 = (bf16[96,1024]{1,0:T(8,128)(2,1)S(1)}, bf16[96,1024]{1,0:T(8,128)(2,1)S(1)}, u32[]{:S(2)}, u32[]{:S(2)}) collective-permute-start(bf16[96,1024]{1,0:T(8,128)(2,1)S(1)} %get-tuple-element.19), channel_id=1, source_target_pairs={{0,16},{1,17},{2,18},{3,19},{4,20},{5,21},{6,22},{7,23},{8,24},{9,... | collective-permute-start | bytes 589832 | tf_op jit(solution)/shard_map/ppermute | solution.py:47
  37.3 5.1 %collective-permute-start.7 = (bf16[96,1024]{1,0:T(8,128)(2,1)S(1)}, bf16[96,1024]{1,0:T(8,128)(2,1)S(1)}, u32[]{:S(2)}, u32[]{:S(2)}) collective-permute-start(bf16[96,1024]{1,0:T(8,128)(2,1)S(1)} %get-tuple-element.18), channel_id=1, source_target_pairs={{0,2},{1,3},{2,0},{3,1},{4,6},{5,7},{6,4},{7,5},{8,10},{9,11},{10,... | collective-permute-start | bytes 589832 | tf_op jit(solution)/shard_map/ppermute | solution.py:47
  38.8 6.8 %collective-permute-start.8 = (bf16[96,1024]{1,0:T(8,128)(2,1)S(1)}, bf16[96,1024]{1,0:T(8,128)(2,1)S(1)}, u32[]{:S(2)}, u32[]{:S(2)}) collective-permute-start(bf16[96,1024]{1,0:T(8,128)(2,1)S(1)} %get-tuple-element.18), channel_id=1, source_target_pairs={{0,6},{1,7},{2,4},{3,5},{4,2},{5,3},{6,0},{7,1},{8,14},{9,15},{10,... | collective-permute-start | bytes 589832 | tf_op jit(solution)/shard_map/ppermute | solution.py:47
  45.6 4.4 %copy-start.1 = (bf16[2048,448]{1,0:T(8,128)(2,1)S(1)}, bf16[2048,448]{1,0:T(8,128)(2,1)}, u32[]{:S(2)}) copy-start(bf16[2048,448]{1,0:T(8,128)(2,1)} %copy-done) | copy-start | bytes 5505028
  45.6 14.3 %collective-permute-start.12 = (bf16[384,1024]{1,0:T(8,128)(2,1)S(1)}, bf16[384,1024]{1,0:T(8,128)(2,1)S(1)}, u32[]{:S(2)}, u32[]{:S(2)}) collective-permute-start(bf16[384,1024]{1,0:T(8,128)(2,1)S(1)} %shard_map.47.piece), channel_id=1, source_target_pairs={{0,1},{1,0},{2,3},{3,2},{4,5},{5,4},{6,7},{7,6},{8,9},{9,8},{10,11... | collective-permute-start | bytes 2359304 | tf_op jit(solution)/shard_map/ppermute | solution.py:47

commit v2 on v1

--- a/solution.py
+++ b/solution.py
@@ -9,24 +9,23 @@
 
 
 SR = 16
-LEVELS = 5
 LEAF = 48
 PAIR = 2 * SR
 AXES = ("row", "sub")
 
 
-OWN = [(0, l) for l in (1, 2, 3, 4, 5)]
+LAID = (1, 2, 4, 5, 3)
+OWN = [(0, l) for l in LAID]
 FIRST = (
-    [(2, l) for l in (2, 3, 4, 5)]
-    + [(6, l) for l in (3, 4, 5)]
-    + [(4, l) for l in (3, 4, 5)]
+    [(m, l) for m in (2, 6) for l in (5, 3)]
+    + [(4, l) for l in (4, 5)]
     + [(16, 5)]
     + [(8, l) for l in (4, 5)]
     + [(24, 5)]
 )
 SECOND = (
-    [(10, 4), (10, 5), (26, 5)]
-    + [(14, 4), (14, 5), (30, 5)]
+    [(10, 4), (10, 5), (26, 5), (2, 2), (2, 4)]
+    + [(14, 4), (14, 5), (30, 5), (4, 3), (6, 4)]
     + [(12, 4), (12, 5)]
     + [(18, 5), (22, 5), (20, 5)]
     + [(28, 5)]
@@ -36,11 +35,17 @@
 
 GRANT = 20 << 20
 SMALL = 6 << 20
-TILES = (2048,)
-LAST_TILES = (1024, 768, 256)
+TILES = (1024, 1024)
+LAST_TILES = (768, 768, 512)
+EARLY = 1024
 
 VMEM = pl.BlockSpec(memory_space=pltpu.VMEM)
+HBM = pl.BlockSpec(memory_space=pltpu.HBM)
 ANY = pl.BlockSpec(memory_space=pl.ANY)
+
+
+def in_hbm(value):
+    return pltpu.with_memory_space_constraint(value, pltpu.HBM)
 
 
 def exchange(value, mask):
@@ -51,8 +56,10 @@
     return pltpu.CompilerParams(vmem_limit_bytes=limit)
 
 
-def arrange_kernel(count, mine, theirs, blocks, *refs):
-    outs, pick, rows, sem = refs[:-3], refs[-3], refs[-2], refs[-1]
+def arrange_kernel(count, mine_hbm, theirs, blocks, *refs):
+    outs, (pick, rows, mine, sem) = refs[:-4], refs[-4:]
+    own_map = pltpu.make_async_copy(mine_hbm, mine, sem.at[len(DEPTHS)])
+    own_map.start()
     device = lax.axis_index("row") * lax.axis_size("sub") + lax.axis_index("sub")
     at, waits = 0, []
     for number, chunk in enumerate(CHUNKS):
@@ -74,6 +81,7 @@
         for copy in copies:
             copy.start()
         waits.append(copies)
+    own_map.wait()
     upper = lax.axis_index("sub") % 2 == 1
     local = lax.broadcasted_iota(jnp.int32, pick.shape[1:], 0)
     for core in range(2):
@@ -102,19 +110,20 @@
         + [pltpu.VMEM((2, kept, kept), jnp.bfloat16)],
         in_specs=[
             pl.BlockSpec(memory_space=pltpu.SMEM),
+            HBM,
             VMEM,
-            VMEM,
-            pl.BlockSpec(memory_space=pltpu.HBM),
+            HBM,
         ],
         out_specs=[VMEM] * (len(DEPTHS) + 1),
         scratch_shapes=[
             pltpu.VMEM(blocks.shape, jnp.bfloat16),
-            pltpu.SemaphoreType.DMA((len(DEPTHS),)),
+            pltpu.VMEM(mine.shape, mine.dtype),
+            pltpu.SemaphoreType.DMA((len(DEPTHS) + 1,)),
         ],
         compiler_params=params(GRANT),
         cost_estimate=pl.CostEstimate(flops=0, bytes_accessed=9 << 20, transcendentals=0),
         name="arrange",
-    )(leaf_count, mine, theirs, pltpu.with_memory_space_constraint(blocks, pltpu.HBM))
+    )(leaf_count, in_hbm(mine), theirs, in_hbm(blocks))
 
 
 def place_kernel(pick, blocks, _, own, swap):
@@ -133,9 +142,9 @@
         )
         own[:LEAF, columns] = jnp.where(upper, odd[:LEAF], even[:LEAF]).astype(jnp.bfloat16)
         swap[:LEAF, columns] = jnp.where(upper, even[:LEAF], odd[:LEAF]).astype(jnp.bfloat16)
-        for level in range(LEVELS):
-            source = slice(LEAF + level * SR, LEAF + (level + 1) * SR)
-            target = LEAF + level * PAIR
+        for place, level in enumerate(LAID):
+            source = slice(LEAF + (level - 1) * SR, LEAF + level * SR)
+            target = LEAF + place * PAIR
             for value in (even, odd):
                 share = value[source].astype(jnp.bfloat16)
                 own[target : target + SR, columns] = share
@@ -156,13 +165,17 @@
     )(pick, blocks, after)
 
 
+def cut(piece, start, stop):
+    return (piece.shape[0] if stop is None else stop) - start
+
+
 def collect_kernel(parts, *refs):
     count = len(refs) - len(parts)
     for part, out in zip(parts, refs[count:]):
         at = 0
-        for index, start in part:
-            depth = refs[index].shape[0] - start
-            out[at : at + depth, :] = refs[index][start:, :]
+        for index, start, stop in part:
+            depth = cut(refs[index], start, stop)
+            out[at : at + depth, :] = refs[index][start : start + depth, :]
             at += depth
 
 
@@ -171,7 +184,7 @@
     return pl.pallas_call(
         functools.partial(collect_kernel, parts),
         out_shape=[
-            pltpu.VMEM((sum(pieces[i].shape[0] - s for i, s in part), width), jnp.bfloat16)
+            pltpu.VMEM((sum(cut(pieces[i], a, b) for i, a, b in part), width), jnp.bfloat16)
             for part in parts
         ],
         in_specs=[VMEM] * len(pieces),
@@ -189,14 +202,12 @@
 
 def product_kernel(first, modes, own, got, *refs):
     total = refs[-1]
-    width = own.shape[1]
-    for lane, piece in enumerate((own, got)):
-        columns = slice(lane * width, (lane + 1) * width)
-        for rows in spans(TILES):
-            value = jnp.dot(modes[rows, :], piece[...], preferred_element_type=jnp.float32)
-            if not first:
-                value = value + refs[0][rows, columns]
-            total[rows, columns] = value
+    piece = jnp.concatenate([own[...], got[...]], axis=1)
+    for rows in spans(TILES):
+        value = jnp.dot(modes[rows, :], piece, preferred_element_type=jnp.float32)
+        if not first:
+            value = value + refs[0][rows, :]
+        total[rows, :] = value
 
 
 def product(modes, own, got, total=None):
@@ -216,44 +227,76 @@
     )(*operands)
 
 
-def finish_kernel(lane, modes, piece, total, *refs):
-    out, buf, sem = refs[-3:]
+def lane_sends(source, at, rows, out, core, sem):
+    depth = rows.stop - rows.start
+    return [
+        pltpu.make_async_copy(
+            source.at[at : at + depth, part * 128 : (part + 1) * 128],
+            out.at[rows, pl.ds(pl.multiple_of((2 * part + core) * 128, 128), 128)],
+            sem,
+        )
+        for part in range(source.shape[1] // 128)
+    ]
+
+
+def own_lane_kernel(modes, piece, total, out, rest, buf, sem):
+    core = lax.axis_index("sub") % 2
     width = piece.shape[1]
-    columns = slice(lane * width, (lane + 1) * width)
+    early, late = spans((buf.shape[0], rest.shape[0]))
+    sends = []
+    for rows, target in ((early, buf), (late, rest)):
+        value = jnp.dot(modes[rows, :], piece[...], preferred_element_type=jnp.float32)
+        target[...] = (value + total[rows, :width]).astype(jnp.bfloat16)
+        if target is buf:
+            sends = lane_sends(buf, 0, rows, out, core, sem)
+            for send in sends:
+                send.start()
+    for send in sends:
+        send.wait()
+
+
+def last_kernel(modes, piece, total, rest, _, out, buf, sem):
     core = lax.axis_index("sub") % 2
-    core = 1 - core if lane else core
-    sends = []
+    width = piece.shape[1]
+    late = slice(modes.shape[0] - rest.shape[0], modes.shape[0])
+    started = lane_sends(rest, 0, late, out, core, sem.at[len(LAST_TILES)])
+    for send in started:
+        send.start()
     for number, rows in enumerate(spans(LAST_TILES)):
         value = jnp.dot(modes[rows, :], piece[...], preferred_element_type=jnp.float32)
-        buf[rows, :] = (value + total[rows, columns]).astype(jnp.bfloat16)
-        for part in range(width // 128):
-            target = pl.multiple_of((2 * part + core) * 128, 128)
-            sends.append(
-                pltpu.make_async_copy(
-                    buf.at[rows, part * 128 : (part + 1) * 128],
-                    out.at[rows, pl.ds(target, 128)],
-                    sem.at[number],
-                )
-            )
-            sends[-1].start()
-    for send in sends:
+        buf[rows, :] = (value + total[rows, width:]).astype(jnp.bfloat16)
+        for send in lane_sends(buf, rows.start, rows, out, 1 - core, sem.at[number]):
+            send.start()
+            started.append(send)
+    for send in started:
         send.wait()
 
 
-def finish(lane, modes, piece, total, out=None):
+def finish(modes, piece, total, before=None):
     ndof, depth = modes.shape
     width = piece.shape[1]
-    operands = [modes, piece, total] + ([] if out is None else [out])
-    return pl.pallas_call(
-        functools.partial(finish_kernel, lane),
-        out_shape=jax.ShapeDtypeStruct((ndof, 2 * width), jnp.bfloat16),
-        in_specs=[VMEM] * 3 + [ANY] * (len(operands) - 3),
-        out_specs=ANY,
-        scratch_shapes=[
+    out = jax.ShapeDtypeStruct((ndof, 2 * width), jnp.bfloat16)
+    if before is None:
+        kernel, operands = own_lane_kernel, [modes, piece, total]
+        out_shape = [out, pltpu.VMEM((ndof - EARLY, width), jnp.bfloat16)]
+        out_specs, alias = [ANY, VMEM], {}
+        in_specs = [VMEM] * 3
+        scratch = [pltpu.VMEM((EARLY, width), jnp.bfloat16), pltpu.SemaphoreType.DMA]
+    else:
+        kernel, operands = last_kernel, [modes, piece, total, before[1], before[0]]
+        out_shape, out_specs, alias = out, ANY, {4: 0}
+        in_specs = [VMEM] * 4 + [ANY]
+        scratch = [
             pltpu.VMEM((ndof, width), jnp.bfloat16),
-            pltpu.SemaphoreType.DMA((len(LAST_TILES),)),
-        ],
-        input_output_aliases={} if out is None else {3: 0},
+            pltpu.SemaphoreType.DMA((len(LAST_TILES) + 1,)),
+        ]
+    return pl.pallas_call(
+        kernel,
+        out_shape=out_shape,
+        in_specs=in_specs,
+        out_specs=out_specs,
+        scratch_shapes=scratch,
+        input_output_aliases=alias,
         compiler_params=params(GRANT),
         cost_estimate=pl.CostEstimate(
             flops=2 * ndof * width * depth, bytes_accessed=8 << 20, transcendentals=0
@@ -274,40 +317,43 @@
         tiled=True,
         axis_index_groups=lanes,
     )
-    own, swap = place(pick, blocks, modes[0])
-
-    def shares(low):
-        return own[LEAF + (low - 1) * PAIR :]
+    own, swap = place(pick, blocks, modes[2])
+
+    def shares(low, high):
+        at = LEAF + PAIR * LAID.index(low)
+        return slice(at, LEAF + PAIR * (LAID.index(high) + 1))
 
     got = exchange(swap, 1)
-    f = exchange(shares(2), 2)
-    g = exchange(shares(3), 6)
-    h = exchange(shares(3), 4)
-    z = exchange(shares(4), 8)
-    x = exchange(shares(5), 16)
-    xz = exchange(shares(5), 24)
+    f = exchange(own[shares(5, 3)], 2)
+    g = exchange(own[shares(5, 3)], 6)
+    h = exchange(own[shares(4, 5)], 4)
+    z = exchange(own[shares(4, 5)], 8)
+    x = exchange(own[shares(5, 5)], 16)
+    xz = exchange(own[shares(5, 5)], 24)
     total = product(modes[0], own, got)
-    own, along_y, along_x = collect(
-        [f, g, h, x, z, xz],
+    extra_f, extra_g = shares(2, 4), shares(4, 4)
+    first, along_f, along_g, along_x = collect(
+        [f, g, h, x, z, xz, own],
         [
-            [(i, 0) for i in range(6)],
-            [(4, 0), (5, 0)],
-            [(0, 3 * PAIR), (1, 2 * PAIR), (2, 2 * PAIR)],
+            [(i, 0, None) for i in range(6)],
+            [(4, 0, None), (5, 0, None), (6, extra_f.start, extra_f.stop)],
+            [(4, 0, None), (5, 0, None), (0, PAIR, None), (6, extra_g.start, extra_g.stop)],
+            [(0, 0, PAIR), (1, 0, PAIR), (2, PAIR, None)],
         ],
     )
-    second = [
-        exchange(along_y, 2),
-        exchange(along_y, 6),
-        exchange(h[PAIR:], 8),
+    pieces = [
+        exchange(along_f, 2),
+        exchange(along_g, 6),
+        exchange(h, 8),
         exchange(along_x, 16),
-        exchange(h[2 * PAIR :], 24),
+        exchange(h[PAIR:], 24),
     ]
-    got = exchange(own, 1)
-    total = product(modes[1], own, got, total)
-    (own,) = collect(second, [[(i, 0) for i in range(5)]])
-    got = exchange(own, 1)
-    out = finish(0, modes[2], own, total)
-    return finish(1, modes[2], got, total, out)
+    got = exchange(first, 1)
+    total = product(modes[1], first, got, total)
+    (last,) = collect(pieces, [[(i, 0, None) for i in range(5)]])
+    got = exchange(last, 1)
+    full = finish(modes[2], last, total)
+    return finish(modes[2], got, total, full)
 
 
 def solution(mesh):

time: 63.7 us -> 57.7 us (0.906)
  waiting for transfers between devices: 18 us -> 13.7 us
  Pallas kernels: 19 us -> 17.4 us
  starting transfers between devices: 23.5 us -> 22 us
  local copies, waits for them, and re-layouts: 2.04 us -> 3.4 us
    ppermute x15, waiting for transfers between devices: 14.6 us -> 10.4 us  [exchange(): return lax.ppermute(value, AXES, [(i, i ^ mask) for i in range(128)])]
    ppermute x15, starting transfers between devices: 17.2 us -> 15.6 us  [exchange(): return lax.ppermute(value, AXES, [(i, i ^ mask) for i in range(128)])]
    pallas_call x2, Pallas kernels: 8.91 us -> 7.41 us  [product(): pl.pallas_call(functools.partial(product_kernel, total is None), out_shap...]
    unnamed x6 -> x8, local copies, waits for them, and re-layouts: 1.97 us -> 3.37 us
  transfers between devices with their start and end apart: 16 -> 16, of which waited for: 10 -> 6; matrix products, arithmetic and copies ran while one was open for 0% -> 0% of each run, Pallas kernels for 24% -> 24%
where the time goes in v2:
time: 57.7 us; the launch traced here: 57.4 us
  starting transfers between devices  22 us (38%)
  Pallas kernels  17.4 us (30%)
  waiting for transfers between devices  13.7 us (24%)
  local copies, waits for them, and re-layouts  3.4 us (6%)
  between operations  0.94 us (2%)
    ppermute x15, starting transfers between devices, exchange(): return lax.ppermute(value, AXES, [(i, i ^ mask) for i in range(128)])  15.6 us
    ppermute x15, waiting for transfers between devices, exchange(): return lax.ppermute(value, AXES, [(i, i ^ mask) for i in range(128)])  10.4 us
    pallas_call x2, Pallas kernels, product(): pl.pallas_call(functools.partial(product_kernel, total is None), out_shap...  7.41 us
    pallas_call x2, Pallas kernels, finish(): pl.pallas_call(kernel, out_shape=out_shape, in_specs=in_specs, out_specs=...  6.6 us
    all_to_all x1, starting transfers between devices, shards(): lax.all_to_all(ritz_coefficients.reshape(parts, -1, width), 'sub', split_...  6.36 us
    unnamed x8, local copies, waits for them, and re-layouts  3.37 us
    all_to_all x1, waiting for transfers between devices, shards(): lax.all_to_all(ritz_coefficients.reshape(parts, -1, width), 'sub', split_...  3.28 us
    pallas_call x1, Pallas kernels, arrange(): pl.pallas_call(arrange_kernel, out_shape=[pltpu.VMEM((ndof, depth), jnp.b...  2.9 us
  transfers between devices with their start and end apart: 16, of which 6 were waited for; matrix products, arithmetic and copies ran while one was open for 0% of the time, Pallas kernels for 24%

profile of v2, /device:TPU:1, one launch (start us, length us, event | category | flops | bytes accessed | tf_op | source)
XLA Modules:
  0.0 57.4 jit_solution(14090740013402851670)
XLA Ops:
  0.0 6.4 %all-to-all-start = ((bf16[8,256,128]{2,1,0:T(8,128)(2,1)}), bf16[8,256,128]{2,1,0:T(8,128)(2,1)S(1)}, u32[]{:S(2)}, u32[]{:S(2)}) async-start(bf16[8,256,128]{2,1,0:T(8,128)(2,1)} %bitcast.1), calls=%async_computation | async-start | bytes 1048576 | tf_op jit(solution)/shard_map/all_to_all | solution.py:312
  6.4 1.0 %collective-permute-start = (s32[1,128]{1,0:T(1,128)}, s32[1,128]{1,0:T(1,128)S(1)}, u32[]{:S(2)}, u32[]{:S(2)}) collective-permute-start(s32[1,128]{1,0:T(1,128)} %mine_hbm.1), channel_id=1, source_target_pairs={{0,1},{1,0},{2,3},{3,2},{4,5},{5,4},{6,7},{7,6},{8,9},{9,8},{10,11... | collective-permute-start | bytes 1544 | tf_op jit(solution)/shard_map/ppermute | solution.py:52
  8.0 0.3 collective-permute-done.theirs
  8.3 2.9 %arrange.1 = (bf16[2048,208]{1,0:T(8,128)(2,1)S(1)}, bf16[2048,320]{1,0:T(8,128)(2,1)S(1)}, bf16[2048,512]{1,0:T(8,128)(2,1)S(1)}, bf16[2,128,128]{2,1,0:T(8,128)(2,1)S(1)}) custom-call(s32[1]{0:T(128)S(6)} %copy.9.count, s32[1,128]{1,0:T(1,128)} %mine_hbm.1, s32[1,128]{1,0:T(1,128)S(1)} %collective-permute-done.theirs, bf16[1040,2048]{1,0:T(8,128)(2,1)} %blocks.1), custom_call_target="tpu_custom_call" | custom-call | bytes 9437184 | tf_op jit(solution)/shard_map/arrange/pallas_call | solution.py:107
  11.2 1.1 %copy-done = bf16[2048,320]{1,0:T(8,128)(2,1)} copy-done((bf16[2048,320]{1,0:T(8,128)(2,1)}, bf16[2048,320]{1,0:T(8,128)(2,1)S(1)}, u32[]{:S(2)}) %copy-start) | copy-done | bytes 1310744
  12.3 1.0 %copy-done.2 = bf16[2048,208]{1,0:T(8,128)(2,1)} copy-done((bf16[2048,208]{1,0:T(8,128)(2,1)}, bf16[2048,208]{1,0:T(8,128)(2,1)S(1)}, u32[]{:S(2)}) %copy-start.2) | copy-done | bytes 851992
  13.3 3.3 %all-to-all-done.blocks = bf16[8,256,128]{2,1,0:T(8,128)(2,1)S(1)} async-done(((bf16[8,256,128]{2,1,0:T(8,128)(2,1)}), bf16[8,256,128]{2,1,0:T(8,128)(2,1)S(1)}, u32[]{:S(2)}, u32[]{:S(2)}) %all-to-all-start) | async-done | bytes 524320 | tf_op jit(solution)/shard_map/all_to_all | solution.py:312
  16.6 0.4 place.1
  17.0 1.3 %collective-permute-start.4 = (bf16[32,1024]{1,0:T(8,128)(2,1)S(1)}, bf16[32,1024]{1,0:T(8,128)(2,1)S(1)}, u32[]{:S(2)}, u32[]{:S(2)}) collective-permute-start(bf16[32,1024]{1,0:T(8,128)(2,1)S(1)} %slice.17), channel_id=1, source_target_pairs={{0,16},{1,17},{2,18},{3,19},{4,20},{5,21},{6,22},{7,23},{8,24},{9,... | collective-permute-start | bytes 196616 | tf_op jit(solution)/shard_map/ppermute | solution.py:52
  18.3 0.5 collective-permute-start.3
  18.8 2.8 %collective-permute-start.2 = (bf16[64,1024]{1,0:T(8,128)(2,1)S(1)}, bf16[64,1024]{1,0:T(8,128)(2,1)S(1)}, u32[]{:S(2)}, u32[]{:S(2)}) collective-permute-start(bf16[64,1024]{1,0:T(8,128)(2,1)S(1)} %get-tuple-element.30), channel_id=1, source_target_pairs={{0,6},{1,7},{2,4},{3,5},{4,2},{5,3},{6,0},{7,1},{8,14},{9,15},{10,... | collective-permute-start | bytes 393224 | tf_op jit(solution)/shard_map/ppermute | solution.py:52
  21.6 0.3 collective-permute-start.5
  21.9 1.2 %collective-permute-start.6 = (bf16[32,1024]{1,0:T(8,128)(2,1)S(1)}, bf16[32,1024]{1,0:T(8,128)(2,1)S(1)}, u32[]{:S(2)}, u32[]{:S(2)}) collective-permute-start(bf16[32,1024]{1,0:T(8,128)(2,1)S(1)} %slice.17), channel_id=1, source_target_pairs={{0,24},{1,25},{2,26},{3,27},{4,28},{5,29},{6,30},{7,31},{8,16},{9,... | collective-permute-start | bytes 196616 | tf_op jit(solution)/shard_map/ppermute | solution.py:52
  23.0 3.2 %collective-permute-done.6.refs_5_ = bf16[32,1024]{1,0:T(8,128)(2,1)S(1)} collective-permute-done((bf16[32,1024]{1,0:T(8,128)(2,1)S(1)}, bf16[32,1024]{1,0:T(8,128)(2,1)S(1)}, u32[]{:S(2)}, u32[]{:S(2)}) %collective-permute-start.6) | collective-permute-done | bytes 65568 | tf_op jit(solution)/shard_map/ppermute | solution.py:52
  26.2 1.1 %collective-permute-done.2.refs_1_ = bf16[64,1024]{1,0:T(8,128)(2,1)S(1)} collective-permute-done((bf16[64,1024]{1,0:T(8,128)(2,1)S(1)}, bf16[64,1024]{1,0:T(8,128)(2,1)S(1)}, u32[]{:S(2)}, u32[]{:S(2)}) %collective-permute-start.2) | collective-permute-done | bytes 131104 | tf_op jit(solution)/shard_map/ppermute | solution.py:52
  27.3 0.1 shard_map.46
  27.4 0.1 collective-permute-start.7
  27.5 1.0 %collective-permute-start.8 = (bf16[160,1024]{1,0:T(8,128)(2,1)S(1)}, bf16[160,1024]{1,0:T(8,128)(2,1)S(1)}, u32[]{:S(2)}, u32[]{:S(2)}) collective-permute-start(bf16[160,1024]{1,0:T(8,128)(2,1)S(1)} %get-tuple-element.21), channel_id=1, source_target_pairs={{0,6},{1,7},{2,4},{3,5},{4,2},{5,3},{6,0},{7,1},{8,14},{9,15},{10,... | collective-permute-start | bytes 983048 | tf_op jit(solution)/shard_map/ppermute | solution.py:52
  28.5 0.3 collective-permute-start.10
  28.7 0.8 %collective-permute-start.9 = (bf16[64,1024]{1,0:T(8,128)(2,1)S(1)}, bf16[64,1024]{1,0:T(8,128)(2,1)S(1)}, u32[]{:S(2)}, u32[]{:S(2)}) collective-permute-start(bf16[64,1024]{1,0:T(8,128)(2,1)S(1)} %collective-permute-done.3.refs_2_), channel_id=1, source_target_pairs={{0,8},{1,9},{2,10},{3,11},{4,12},{5,13},{6,14},{7,15},{8,0},{9,1},... | collective-permute-start | bytes 393224 | tf_op jit(solution)/shard_map/ppermute | solution.py:52
  29.6 1.6 %collective-permute-start.11 = (bf16[32,1024]{1,0:T(8,128)(2,1)S(1)}, bf16[32,1024]{1,0:T(8,128)(2,1)S(1)}, u32[]{:S(2)}, u32[]{:S(2)}) collective-permute-start(bf16[32,1024]{1,0:T(8,128)(2,1)S(1)} %slice.19), channel_id=1, source_target_pairs={{0,24},{1,25},{2,26},{3,27},{4,28},{5,29},{6,30},{7,31},{8,16},{9,... | collective-permute-start | bytes 196616 | tf_op jit(solution)/shard_map/ppermute | solution.py:52
  31.1 3.1 %collective-permute-done.11.refs_4_ = bf16[32,1024]{1,0:T(8,128)(2,1)S(1)} collective-permute-done((bf16[32,1024]{1,0:T(8,128)(2,1)S(1)}, bf16[32,1024]{1,0:T(8,128)(2,1)S(1)}, u32[]{:S(2)}, u32[]{:S(2)}) %collective-permute-start.11) | collective-permute-done | bytes 65568 | tf_op jit(solution)/shard_map/ppermute | solution.py:52
  34.3 3.9 %collective-permute-start.13 = (bf16[320,1024]{1,0:T(8,128)(2,1)S(1)}, bf16[320,1024]{1,0:T(8,128)(2,1)S(1)}, u32[]{:S(2)}, u32[]{:S(2)}) collective-permute-start(bf16[320,1024]{1,0:T(8,128)(2,1)S(1)} %get-tuple-element.24.own), channel_id=1, source_target_pairs={{0,1},{1,0},{2,3},{3,2},{4,5},{5,4},{6,7},{7,6},{8,9},{9,8},{10,11... | collective-permute-start | bytes 1966088 | tf_op jit(solution)/shard_map/ppermute | solution.py:52
  38.2 0.1 shard_map.47.piece
  38.3 0.8 %collective-permute-start.12 = (bf16[512,1024]{1,0:T(8,128)(2,1)S(1)}, bf16[512,1024]{1,0:T(8,128)(2,1)S(1)}, u32[]{:S(2)}, u32[]{:S(2)}) collective-permute-start(bf16[512,1024]{1,0:T(8,128)(2,1)S(1)} %shard_map.47.piece), channel_id=1, source_target_pairs={{0,1},{1,0},{2,3},{3,2},{4,5},{5,4},{6,7},{7,6},{8,9},{9,8},{10,11... | collective-permute-start | bytes 3145736 | tf_op jit(solution)/shard_map/ppermute | solution.py:52
  39.1 0.3 collective-permute-start.14
  39.3 2.7 %collective-permute-done.14.got = bf16[208,1024]{1,0:T(8,128)(2,1)S(1)} collective-permute-done((bf16[208,1024]{1,0:T(8,128)(2,1)S(1)}, bf16[208,1024]{1,0:T(8,128)(2,1)S(1)}, u32[]{:S(2)}, u32[]{:S(2)}) %collective-permute-start.14) | collective-permute-done | bytes 426016 | tf_op jit(solution)/shard_map/ppermute | solution.py:52
  42.0 1.2 %copy-done.3 = bf16[2048,208]{1,0:T(8,128)(2,1)S(1)} copy-done((bf16[2048,208]{1,0:T(8,128)(2,1)S(1)}, bf16[2048,208]{1,0:T(8,128)(2,1)}, u32[]{:S(2)}) %copy-start.3) | copy-done | bytes 851992
  43.2 2.3 %shard_map.48.refs_0_ = f32[2048,2048]{1,0:T(8,128)S(1)} custom-call(bf16[2048,208]{1,0:T(8,128)(2,1)S(1)} %copy-done.3, bf16[208,1024]{1,0:T(8,128)(2,1)S(1)} %get-tuple-element.19.refs_6_.own, bf16[208,1024]{1,0:T(8,128)(2,1)S(1)} %collective-permute-done.14.got), custom_call_target="tpu_custom_call" | custom-call | flops 1744830464 | bytes 8388608 | tf_op jit(solution)/shard_map/pallas_call | solution.py:217
  45.6 5.1 %shard_map.49.total = f32[2048,2048]{1,0:T(8,128)S(1)} custom-call(bf16[2048,320]{1,0:T(8,128)(2,1)S(1)} %copy-done.1, bf16[320,1024]{1,0:T(8,128)(2,1)S(1)} %get-tuple-element.24.own, bf16[320,1024]{1,0:T(8,128)(2,1)S(1)} %collective-permute-done.13.got, f32[2048,2048]{1,0:T(8,128)S(1)} %shard_map.48.refs_0_), custom_call_target="tpu_custom_call", output_to_operand_aliasing={{}: (3, {})} | custom-call | flops 2684354560 | bytes 8388608 | tf_op jit(solution)/shard_map/pallas_call | solution.py:217
  50.7 3.3 %shard_map.50 = (bf16[2048,2048]{1,0:T(8,128)(2,1)}, bf16[1024,1024]{1,0:T(8,128)(2,1)S(1)}) custom-call(bf16[2048,512]{1,0:T(8,128)(2,1)S(1)} %get-tuple-element.17._.modes, bf16[512,1024]{1,0:T(8,128)(2,1)S(1)} %shard_map.47.piece, f32[2048,2048]{1,0:T(8,128)S(1)} %shard_map.49.total), custom_call_target="tpu_custom_call" | custom-call | flops 2147483648 | bytes 8388608 | tf_op jit(solution)/shard_map/pallas_call | solution.py:293
  54.0 3.3 %shard_map.51 = bf16[2048,2048]{1,0:T(8,128)(2,1)} custom-call(bf16[2048,512]{1,0:T(8,128)(2,1)S(1)} %get-tuple-element.17._.modes, bf16[512,1024]{1,0:T(8,128)(2,1)S(1)} %collective-permute-done.12.piece, f32[2048,2048]{1,0:T(8,128)S(1)} %shard_map.49.total, bf16[1024,1024]{1,0:T(8,128)(2,1)S(1)} %get-tuple-element.27.rest, ...), custom_call_target="tpu_custom_call", output_to_operand_aliasing={{}: (4, {})} | custom-call | flops 2147483648 | bytes 8388608 | tf_op jit(solution)/shard_map/pallas_call | solution.py:293
  (19 shorter events, 0.1 us)
Async XLA Ops:
  0.0 16.6 %all-to-all-start = ((bf16[8,256,128]{2,1,0:T(8,128)(2,1)}), bf16[8,256,128]{2,1,0:T(8,128)(2,1)S(1)}, u32[]{:S(2)}, u32[]{:S(2)}) async-start(bf16[8,256,128]{2,1,0:T(8,128)(2,1)} %bitcast.1), calls=%async_computation | async-start | bytes 1048576 | tf_op jit(solution)/shard_map/all_to_all | solution.py:312
  6.4 1.9 %collective-permute-start = (s32[1,128]{1,0:T(1,128)}, s32[1,128]{1,0:T(1,128)S(1)}, u32[]{:S(2)}, u32[]{:S(2)}) collective-permute-start(s32[1,128]{1,0:T(1,128)} %mine_hbm.1), channel_id=1, source_target_pairs={{0,1},{1,0},{2,3},{3,2},{4,5},{5,4},{6,7},{7,6},{8,9},{9,8},{10,11... | collective-permute-start | bytes 1544 | tf_op jit(solution)/shard_map/ppermute | solution.py:52
  11.2 1.1 %copy-start = (bf16[2048,320]{1,0:T(8,128)(2,1)}, bf16[2048,320]{1,0:T(8,128)(2,1)S(1)}, u32[]{:S(2)}) copy-start(bf16[2048,320]{1,0:T(8,128)(2,1)S(1)} %get-tuple-element.23.modes) | copy-start | bytes 3932164
  12.3 1.0 %copy-start.2 = (bf16[2048,208]{1,0:T(8,128)(2,1)}, bf16[2048,208]{1,0:T(8,128)(2,1)S(1)}, u32[]{:S(2)}) copy-start(bf16[2048,208]{1,0:T(8,128)(2,1)S(1)} %get-tuple-element.25.modes) | copy-start | bytes 2555908
  17.0 4.8 %collective-permute-start.4 = (bf16[32,1024]{1,0:T(8,128)(2,1)S(1)}, bf16[32,1024]{1,0:T(8,128)(2,1)S(1)}, u32[]{:S(2)}, u32[]{:S(2)}) collective-permute-start(bf16[32,1024]{1,0:T(8,128)(2,1)S(1)} %slice.17), channel_id=1, source_target_pairs={{0,16},{1,17},{2,18},{3,19},{4,20},{5,21},{6,22},{7,23},{8,24},{9,... | collective-permute-start | bytes 196616 | tf_op jit(solution)/shard_map/ppermute | solution.py:52
  18.3 7.9 %collective-permute-start.3 = (bf16[64,1024]{1,0:T(8,128)(2,1)S(1)}, bf16[64,1024]{1,0:T(8,128)(2,1)S(1)}, u32[]{:S(2)}, u32[]{:S(2)}) collective-permute-start(bf16[64,1024]{1,0:T(8,128)(2,1)S(1)} %get-tuple-element.29), channel_id=1, source_target_pairs={{0,4},{1,5},{2,6},{3,7},{4,0},{5,1},{6,2},{7,3},{8,12},{9,13},{10,... | collective-permute-start | bytes 393224 | tf_op jit(solution)/shard_map/ppermute | solution.py:52
  18.8 7.4 %collective-permute-start.1 = (bf16[64,1024]{1,0:T(8,128)(2,1)S(1)}, bf16[64,1024]{1,0:T(8,128)(2,1)S(1)}, u32[]{:S(2)}, u32[]{:S(2)}) collective-permute-start(bf16[64,1024]{1,0:T(8,128)(2,1)S(1)} %get-tuple-element.30), channel_id=1, source_target_pairs={{0,2},{1,3},{2,0},{3,1},{4,6},{5,7},{6,4},{7,5},{8,10},{9,11},{10,... | collective-permute-start | bytes 393224 | tf_op jit(solution)/shard_map/ppermute | solution.py:52
  18.8 8.5 %collective-permute-start.2 = (bf16[64,1024]{1,0:T(8,128)(2,1)S(1)}, bf16[64,1024]{1,0:T(8,128)(2,1)S(1)}, u32[]{:S(2)}, u32[]{:S(2)}) collective-permute-start(bf16[64,1024]{1,0:T(8,128)(2,1)S(1)} %get-tuple-element.30), channel_id=1, source_target_pairs={{0,6},{1,7},{2,4},{3,5},{4,2},{5,3},{6,0},{7,1},{8,14},{9,15},{10,... | collective-permute-start | bytes 393224 | tf_op jit(solution)/shard_map/ppermute | solution.py:52
  21.6 5.7 %collective-permute-start.5 = (bf16[64,1024]{1,0:T(8,128)(2,1)S(1)}, bf16[64,1024]{1,0:T(8,128)(2,1)S(1)}, u32[]{:S(2)}, u32[]{:S(2)}) collective-permute-start(bf16[64,1024]{1,0:T(8,128)(2,1)S(1)} %get-tuple-element.29), channel_id=1, source_target_pairs={{0,8},{1,9},{2,10},{3,11},{4,12},{5,13},{6,14},{7,15},{8,0},{9,1},... | collective-permute-start | bytes 393224 | tf_op jit(solution)/shard_map/ppermute | solution.py:52
  21.9 4.3 %collective-permute-start.6 = (bf16[32,1024]{1,0:T(8,128)(2,1)S(1)}, bf16[32,1024]{1,0:T(8,128)(2,1)S(1)}, u32[]{:S(2)}, u32[]{:S(2)}) collective-permute-start(bf16[32,1024]{1,0:T(8,128)(2,1)S(1)} %slice.17), channel_id=1, source_target_pairs={{0,24},{1,25},{2,26},{3,27},{4,28},{5,29},{6,30},{7,31},{8,16},{9,... | collective-permute-start | bytes 196616 | tf_op jit(solution)/shard_map/ppermute | solution.py:52
  27.4 10.8 %collective-permute-start.7 = (bf16[160,1024]{1,0:T(8,128)(2,1)S(1)}, bf16[160,1024]{1,0:T(8,128)(2,1)S(1)}, u32[]{:S(2)}, u32[]{:S(2)}) collective-permute-start(bf16[160,1024]{1,0:T(8,128)(2,1)S(1)} %get-tuple-element.20), channel_id=1, source_target_pairs={{0,2},{1,3},{2,0},{3,1},{4,6},{5,7},{6,4},{7,5},{8,10},{9,11},{10,... | collective-permute-start | bytes 983048 | tf_op jit(solution)/shard_map/ppermute | solution.py:52
  27.5 10.7 %collective-permute-start.8 = (bf16[160,1024]{1,0:T(8,128)(2,1)S(1)}, bf16[160,1024]{1,0:T(8,128)(2,1)S(1)}, u32[]{:S(2)}, u32[]{:S(2)}) collective-permute-start(bf16[160,1024]{1,0:T(8,128)(2,1)S(1)} %get-tuple-element.21), channel_id=1, source_target_pairs={{0,6},{1,7},{2,4},{3,5},{4,2},{5,3},{6,0},{7,1},{8,14},{9,15},{10,... | collective-permute-start | bytes 983048 | tf_op jit(solution)/shard_map/ppermute | solution.py:52
  28.5 9.7 %collective-permute-start.10 = (bf16[96,1024]{1,0:T(8,128)(2,1)S(1)}, bf16[96,1024]{1,0:T(8,128)(2,1)S(1)}, u32[]{:S(2)}, u32[]{:S(2)}) collective-permute-start(bf16[96,1024]{1,0:T(8,128)(2,1)S(1)} %get-tuple-element.22), channel_id=1, source_target_pairs={{0,16},{1,17},{2,18},{3,19},{4,20},{5,21},{6,22},{7,23},{8,24},{9,... | collective-permute-start | bytes 589832 | tf_op jit(solution)/shard_map/ppermute | solution.py:52
  28.7 9.4 %collective-permute-start.9 = (bf16[64,1024]{1,0:T(8,128)(2,1)S(1)}, bf16[64,1024]{1,0:T(8,128)(2,1)S(1)}, u32[]{:S(2)}, u32[]{:S(2)}) collective-permute-start(bf16[64,1024]{1,0:T(8,128)(2,1)S(1)} %collective-permute-done.3.refs_2_), channel_id=1, source_target_pairs={{0,8},{1,9},{2,10},{3,11},{4,12},{5,13},{6,14},{7,15},{8,0},{9,1},... | collective-permute-start | bytes 393224 | tf_op jit(solution)/shard_map/ppermute | solution.py:52
  29.6 4.7 %collective-permute-start.11 = (bf16[32,1024]{1,0:T(8,128)(2,1)S(1)}, bf16[32,1024]{1,0:T(8,128)(2,1)S(1)}, u32[]{:S(2)}, u32[]{:S(2)}) collective-permute-start(bf16[32,1024]{1,0:T(8,128)(2,1)S(1)} %slice.19), channel_id=1, source_target_pairs={{0,24},{1,25},{2,26},{3,27},{4,28},{5,29},{6,30},{7,31},{8,16},{9,... | collective-permute-start | bytes 196616 | tf_op jit(solution)/shard_map/ppermute | solution.py:52
  34.3 11.3 %collective-permute-start.13 = (bf16[320,1024]{1,0:T(8,128)(2,1)S(1)}, bf16[320,1024]{1,0:T(8,128)(2,1)S(1)}, u32[]{:S(2)}, u32[]{:S(2)}) collective-permute-start(bf16[320,1024]{1,0:T(8,128)(2,1)S(1)} %get-tuple-element.24.own), channel_id=1, source_target_pairs={{0,1},{1,0},{2,3},{3,2},{4,5},{5,4},{6,7},{7,6},{8,9},{9,8},{10,11... | collective-permute-start | bytes 1966088 | tf_op jit(solution)/shard_map/ppermute | solution.py:52
  38.3 15.7 %collective-permute-start.12 = (bf16[512,1024]{1,0:T(8,128)(2,1)S(1)}, bf16[512,1024]{1,0:T(8,128)(2,1)S(1)}, u32[]{:S(2)}, u32[]{:S(2)}) collective-permute-start(bf16[512,1024]{1,0:T(8,128)(2,1)S(1)} %shard_map.47.piece), channel_id=1, source_target_pairs={{0,1},{1,0},{2,3},{3,2},{4,5},{5,4},{6,7},{7,6},{8,9},{9,8},{10,11... | collective-permute-start | bytes 3145736 | tf_op jit(solution)/shard_map/ppermute | solution.py:52
  39.1 2.9 %collective-permute-start.14 = (bf16[208,1024]{1,0:T(8,128)(2,1)S(1)}, bf16[208,1024]{1,0:T(8,128)(2,1)S(1)}, u32[]{:S(2)}, u32[]{:S(2)}) collective-permute-start(bf16[208,1024]{1,0:T(8,128)(2,1)S(1)} %get-tuple-element.26), channel_id=1, source_target_pairs={{0,1},{1,0},{2,3},{3,2},{4,5},{5,4},{6,7},{7,6},{8,9},{9,8},{10,11... | collective-permute-start | bytes 1277960 | tf_op jit(solution)/shard_map/ppermute | solution.py:52
  42.0 1.2 %copy-start.3 = (bf16[2048,208]{1,0:T(8,128)(2,1)S(1)}, bf16[2048,208]{1,0:T(8,128)(2,1)}, u32[]{:S(2)}) copy-start(bf16[2048,208]{1,0:T(8,128)(2,1)} %copy-done.2) | copy-start | bytes 2555908
  43.2 2.4 %copy-start.1 = (bf16[2048,320]{1,0:T(8,128)(2,1)S(1)}, bf16[2048,320]{1,0:T(8,128)(2,1)}, u32[]{:S(2)}) copy-start(bf16[2048,320]{1,0:T(8,128)(2,1)} %copy-done) | copy-start | bytes 3932164

commit v3 on v2

--- a/solution.py
+++ b/solution.py
@@ -33,11 +33,13 @@
 CHUNKS = ([None] + OWN, FIRST, SECOND)
 DEPTHS = (LEAF + PAIR * len(OWN), PAIR * len(FIRST), PAIR * len(SECOND))
 
+FAR = 2
+
 GRANT = 20 << 20
 SMALL = 6 << 20
 TILES = (1024, 1024)
 LAST_TILES = (768, 768, 512)
-EARLY = 1024
+EARLY = 256
 
 VMEM = pl.BlockSpec(memory_space=pltpu.VMEM)
 HBM = pl.BlockSpec(memory_space=pltpu.HBM)
@@ -57,7 +59,7 @@
 
 
 def arrange_kernel(count, mine_hbm, theirs, blocks, *refs):
-    outs, (pick, rows, mine, sem) = refs[:-4], refs[-4:]
+    outs, (pick, rows, mine, stage, sem) = refs[:-5], refs[-5:]
     own_map = pltpu.make_async_copy(mine_hbm, mine, sem.at[len(DEPTHS)])
     own_map.start()
     device = lax.axis_index("row") * lax.axis_size("sub") + lax.axis_index("sub")
@@ -97,8 +99,14 @@
             row = lax.broadcasted_iota(jnp.int32, (LEAF, value.shape[1]), 0)
             leaf = jnp.where(row < count[0], value[:LEAF].astype(jnp.float32), 0.0)
             value = jnp.concatenate([leaf.astype(jnp.bfloat16), value[LEAF:]], axis=0)
-        outs[number][...] = value.T
+        if number == FAR:
+            stage[...] = value.T
+            flush = pltpu.make_async_copy(stage, outs[number], sem.at[len(DEPTHS) + 1])
+            flush.start()
+        else:
+            outs[number][...] = value.T
         at += depth
+    flush.wait()
 
 
 def arrange(leaf_count, mine, theirs, blocks):
@@ -106,7 +114,10 @@
     kept = mine.shape[1]
     return pl.pallas_call(
         arrange_kernel,
-        out_shape=[pltpu.VMEM((ndof, depth), jnp.bfloat16) for depth in DEPTHS]
+        out_shape=[
+            (pltpu.HBM if number == FAR else pltpu.VMEM)((ndof, depth), jnp.bfloat16)
+            for number, depth in enumerate(DEPTHS)
+        ]
         + [pltpu.VMEM((2, kept, kept), jnp.bfloat16)],
         in_specs=[
             pl.BlockSpec(memory_space=pltpu.SMEM),
@@ -114,11 +125,12 @@
             VMEM,
             HBM,
         ],
-        out_specs=[VMEM] * (len(DEPTHS) + 1),
+        out_specs=[HBM if number == FAR else VMEM for number in range(len(DEPTHS) + 1)],
         scratch_shapes=[
             pltpu.VMEM(blocks.shape, jnp.bfloat16),
             pltpu.VMEM(mine.shape, mine.dtype),
-            pltpu.SemaphoreType.DMA((len(DEPTHS) + 1,)),
+            pltpu.VMEM((ndof, DEPTHS[FAR]), jnp.bfloat16),
+            pltpu.SemaphoreType.DMA((len(DEPTHS) + 2,)),
         ],
         compiler_params=params(GRANT),
         cost_estimate=pl.CostEstimate(flops=0, bytes_accessed=9 << 20, transcendentals=0),
@@ -317,7 +329,7 @@
         tiled=True,
         axis_index_groups=lanes,
     )
-    own, swap = place(pick, blocks, modes[2])
+    own, swap = place(pick, blocks, modes[0])
 
     def shares(low, high):
         at = LEAF + PAIR * LAID.index(low)

time: 57.7 us -> 56.1 us (0.972)
  local copies, waits for them, and re-layouts: 3.4 us -> 0.04 us
  Pallas kernels: 17.4 us -> 18.5 us
  waiting for transfers between devices: 13.7 us -> 14.5 us
    unnamed x8 -> x2, local copies, waits for them, and re-layouts: 3.37 us -> 0.01 us
    pallas_call x1, Pallas kernels: 2.9 us -> 4.23 us  [arrange(): pl.pallas_call(arrange_kernel, out_shape=[(pltpu.HBM if number == FAR els...]
    all_to_all x1, waiting for transfers between devices: 3.28 us -> 4.11 us  [shards(): lax.all_to_all(ritz_coefficients.reshape(parts, -1, width), 'sub', split_...]
  transfers between devices with their start and end apart: 16 -> 16, of which waited for: 6 -> 6; matrix products, arithmetic and copies ran while one was open for 0% -> 0% of each run, Pallas kernels for 24% -> 26%
where the time goes in v3:
time: 56.1 us; the launch traced here: 55.9 us
  starting transfers between devices  22 us (39%)
  Pallas kernels  18.5 us (33%)
  waiting for transfers between devices  14.5 us (26%)
  between operations  0.94 us (2%)
    ppermute x15, starting transfers between devices, exchange(): return lax.ppermute(value, AXES, [(i, i ^ mask) for i in range(128)])  15.6 us
    ppermute x15, waiting for transfers between devices, exchange(): return lax.ppermute(value, AXES, [(i, i ^ mask) for i in range(128)])  10.4 us
    pallas_call x2, Pallas kernels, product(): pl.pallas_call(functools.partial(product_kernel, total is None), out_shap...  7.39 us
    all_to_all x1, starting transfers between devices, shards(): lax.all_to_all(ritz_coefficients.reshape(parts, -1, width), 'sub', split_...  6.36 us
    pallas_call x2, Pallas kernels, finish(): pl.pallas_call(kernel, out_shape=out_shape, in_specs=in_specs, out_specs=...  6.33 us
    pallas_call x1, Pallas kernels, arrange(): pl.pallas_call(arrange_kernel, out_shape=[(pltpu.HBM if number == FAR els...  4.23 us
    all_to_all x1, waiting for transfers between devices, shards(): lax.all_to_all(ritz_coefficients.reshape(parts, -1, width), 'sub', split_...  4.11 us
  transfers between devices with their start and end apart: 16, of which 6 were waited for; matrix products, arithmetic and copies ran while one was open for 0% of the time, Pallas kernels for 26%

profile of v3, /device:TPU:1, one launch (start us, length us, event | category | flops | bytes accessed | tf_op | source)
XLA Modules:
  0.0 55.9 jit_solution(3928270353855455510)
XLA Ops:
  0.0 6.4 %all-to-all-start = ((bf16[8,256,128]{2,1,0:T(8,128)(2,1)}), bf16[8,256,128]{2,1,0:T(8,128)(2,1)S(1)}, u32[]{:S(2)}, u32[]{:S(2)}) async-start(bf16[8,256,128]{2,1,0:T(8,128)(2,1)} %bitcast.1), calls=%async_computation | async-start | bytes 1048576 | tf_op jit(solution)/shard_map/all_to_all | solution.py:324
  6.4 1.0 %collective-permute-start = (s32[1,128]{1,0:T(1,128)}, s32[1,128]{1,0:T(1,128)S(1)}, u32[]{:S(2)}, u32[]{:S(2)}) collective-permute-start(s32[1,128]{1,0:T(1,128)} %mine_hbm.1), channel_id=1, source_target_pairs={{0,1},{1,0},{2,3},{3,2},{4,5},{5,4},{6,7},{7,6},{8,9},{9,8},{10,11... | collective-permute-start | bytes 1544 | tf_op jit(solution)/shard_map/ppermute | solution.py:54
  8.0 0.3 collective-permute-done.theirs
  8.3 4.2 %arrange.1 = (bf16[2048,208]{1,0:T(8,128)(2,1)S(1)}, bf16[2048,320]{1,0:T(8,128)(2,1)S(1)}, bf16[2048,512]{1,0:T(8,128)(2,1)}, bf16[2,128,128]{2,1,0:T(8,128)(2,1)S(1)}) custom-call(s32[1]{0:T(128)S(6)} %copy.9.count, s32[1,128]{1,0:T(1,128)} %mine_hbm.1, s32[1,128]{1,0:T(1,128)S(1)} %collective-permute-done.theirs, bf16[1040,2048]{1,0:T(8,128)(2,1)} %blocks.1), custom_call_target="tpu_custom_call" | custom-call | bytes 9437184 | tf_op jit(solution)/shard_map/arrange/pallas_call | solution.py:115
  12.5 4.1 %all-to-all-done.blocks = bf16[8,256,128]{2,1,0:T(8,128)(2,1)S(1)} async-done(((bf16[8,256,128]{2,1,0:T(8,128)(2,1)}), bf16[8,256,128]{2,1,0:T(8,128)(2,1)S(1)}, u32[]{:S(2)}, u32[]{:S(2)}) %all-to-all-start) | async-done | bytes 524320 | tf_op jit(solution)/shard_map/all_to_all | solution.py:324
  16.6 0.4 place.1
  17.0 1.3 %collective-permute-start.4 = (bf16[32,1024]{1,0:T(8,128)(2,1)S(1)}, bf16[32,1024]{1,0:T(8,128)(2,1)S(1)}, u32[]{:S(2)}, u32[]{:S(2)}) collective-permute-start(bf16[32,1024]{1,0:T(8,128)(2,1)S(1)} %slice.17), channel_id=1, source_target_pairs={{0,16},{1,17},{2,18},{3,19},{4,20},{5,21},{6,22},{7,23},{8,24},{9,... | collective-permute-start | bytes 196616 | tf_op jit(solution)/shard_map/ppermute | solution.py:54
  18.3 0.5 collective-permute-start.3
  18.8 0.0 collective-permute-start.1
  18.8 2.8 %collective-permute-start.2 = (bf16[64,1024]{1,0:T(8,128)(2,1)S(1)}, bf16[64,1024]{1,0:T(8,128)(2,1)S(1)}, u32[]{:S(2)}, u32[]{:S(2)}) collective-permute-start(bf16[64,1024]{1,0:T(8,128)(2,1)S(1)} %get-tuple-element.30), channel_id=1, source_target_pairs={{0,6},{1,7},{2,4},{3,5},{4,2},{5,3},{6,0},{7,1},{8,14},{9,15},{10,... | collective-permute-start | bytes 393224 | tf_op jit(solution)/shard_map/ppermute | solution.py:54
  21.6 0.3 collective-permute-start.5
  21.9 1.2 %collective-permute-start.6 = (bf16[32,1024]{1,0:T(8,128)(2,1)S(1)}, bf16[32,1024]{1,0:T(8,128)(2,1)S(1)}, u32[]{:S(2)}, u32[]{:S(2)}) collective-permute-start(bf16[32,1024]{1,0:T(8,128)(2,1)S(1)} %slice.17), channel_id=1, source_target_pairs={{0,24},{1,25},{2,26},{3,27},{4,28},{5,29},{6,30},{7,31},{8,16},{9,... | collective-permute-start | bytes 196616 | tf_op jit(solution)/shard_map/ppermute | solution.py:54
  23.0 3.2 %collective-permute-done.6.refs_5_ = bf16[32,1024]{1,0:T(8,128)(2,1)S(1)} collective-permute-done((bf16[32,1024]{1,0:T(8,128)(2,1)S(1)}, bf16[32,1024]{1,0:T(8,128)(2,1)S(1)}, u32[]{:S(2)}, u32[]{:S(2)}) %collective-permute-start.6) | collective-permute-done | bytes 65568 | tf_op jit(solution)/shard_map/ppermute | solution.py:54
  26.2 0.0 collective-permute-done.3.refs_2_
  26.2 1.1 %collective-permute-done.2.refs_1_ = bf16[64,1024]{1,0:T(8,128)(2,1)S(1)} collective-permute-done((bf16[64,1024]{1,0:T(8,128)(2,1)S(1)}, bf16[64,1024]{1,0:T(8,128)(2,1)S(1)}, u32[]{:S(2)}, u32[]{:S(2)}) %collective-permute-start.2) | collective-permute-done | bytes 131104 | tf_op jit(solution)/shard_map/ppermute | solution.py:54
  27.3 0.1 shard_map.46
  27.4 0.1 collective-permute-start.7
  27.5 1.0 %collective-permute-start.8 = (bf16[160,1024]{1,0:T(8,128)(2,1)S(1)}, bf16[160,1024]{1,0:T(8,128)(2,1)S(1)}, u32[]{:S(2)}, u32[]{:S(2)}) collective-permute-start(bf16[160,1024]{1,0:T(8,128)(2,1)S(1)} %get-tuple-element.22), channel_id=1, source_target_pairs={{0,6},{1,7},{2,4},{3,5},{4,2},{5,3},{6,0},{7,1},{8,14},{9,15},{10,... | collective-permute-start | bytes 983048 | tf_op jit(solution)/shard_map/ppermute | solution.py:54
  28.5 0.3 collective-permute-start.10
  28.7 0.8 %collective-permute-start.9 = (bf16[64,1024]{1,0:T(8,128)(2,1)S(1)}, bf16[64,1024]{1,0:T(8,128)(2,1)S(1)}, u32[]{:S(2)}, u32[]{:S(2)}) collective-permute-start(bf16[64,1024]{1,0:T(8,128)(2,1)S(1)} %collective-permute-done.3.refs_2_), channel_id=1, source_target_pairs={{0,8},{1,9},{2,10},{3,11},{4,12},{5,13},{6,14},{7,15},{8,0},{9,1},... | collective-permute-start | bytes 393224 | tf_op jit(solution)/shard_map/ppermute | solution.py:54
  29.6 1.6 %collective-permute-start.11 = (bf16[32,1024]{1,0:T(8,128)(2,1)S(1)}, bf16[32,1024]{1,0:T(8,128)(2,1)S(1)}, u32[]{:S(2)}, u32[]{:S(2)}) collective-permute-start(bf16[32,1024]{1,0:T(8,128)(2,1)S(1)} %slice.19), channel_id=1, source_target_pairs={{0,24},{1,25},{2,26},{3,27},{4,28},{5,29},{6,30},{7,31},{8,16},{9,... | collective-permute-start | bytes 196616 | tf_op jit(solution)/shard_map/ppermute | solution.py:54
  31.1 3.1 %collective-permute-done.11.refs_4_ = bf16[32,1024]{1,0:T(8,128)(2,1)S(1)} collective-permute-done((bf16[32,1024]{1,0:T(8,128)(2,1)S(1)}, bf16[32,1024]{1,0:T(8,128)(2,1)S(1)}, u32[]{:S(2)}, u32[]{:S(2)}) %collective-permute-start.11) | collective-permute-done | bytes 65568 | tf_op jit(solution)/shard_map/ppermute | solution.py:54
  34.3 3.9 %collective-permute-start.13 = (bf16[320,1024]{1,0:T(8,128)(2,1)S(1)}, bf16[320,1024]{1,0:T(8,128)(2,1)S(1)}, u32[]{:S(2)}, u32[]{:S(2)}) collective-permute-start(bf16[320,1024]{1,0:T(8,128)(2,1)S(1)} %get-tuple-element.25.own), channel_id=1, source_target_pairs={{0,1},{1,0},{2,3},{3,2},{4,5},{5,4},{6,7},{7,6},{8,9},{9,8},{10,11... | collective-permute-start | bytes 1966088 | tf_op jit(solution)/shard_map/ppermute | solution.py:54
  38.2 0.1 shard_map.47.piece
  38.3 0.8 %collective-permute-start.12 = (bf16[512,1024]{1,0:T(8,128)(2,1)S(1)}, bf16[512,1024]{1,0:T(8,128)(2,1)S(1)}, u32[]{:S(2)}, u32[]{:S(2)}) collective-permute-start(bf16[512,1024]{1,0:T(8,128)(2,1)S(1)} %shard_map.47.piece), channel_id=1, source_target_pairs={{0,1},{1,0},{2,3},{3,2},{4,5},{5,4},{6,7},{7,6},{8,9},{9,8},{10,11... | collective-permute-start | bytes 3145736 | tf_op jit(solution)/shard_map/ppermute | solution.py:54
  39.1 0.3 collective-permute-start.14
  39.3 2.7 %collective-permute-done.14.got = bf16[208,1024]{1,0:T(8,128)(2,1)S(1)} collective-permute-done((bf16[208,1024]{1,0:T(8,128)(2,1)S(1)}, bf16[208,1024]{1,0:T(8,128)(2,1)S(1)}, u32[]{:S(2)}, u32[]{:S(2)}) %collective-permute-start.14) | collective-permute-done | bytes 426016 | tf_op jit(solution)/shard_map/ppermute | solution.py:54
  42.0 2.3 %shard_map.48.refs_0_ = f32[2048,2048]{1,0:T(8,128)S(1)} custom-call(bf16[2048,208]{1,0:T(8,128)(2,1)S(1)} %get-tuple-element.19._.modes, bf16[208,1024]{1,0:T(8,128)(2,1)S(1)} %get-tuple-element.20.refs_6_.own, bf16[208,1024]{1,0:T(8,128)(2,1)S(1)} %collective-permute-done.14.got), custom_call_target="tpu_custom_call" | custom-call | flops 1744830464 | bytes 8388608 | tf_op jit(solution)/shard_map/pallas_call | solution.py:229
  44.3 0.0 copy-start
  44.4 5.1 %shard_map.49.total = f32[2048,2048]{1,0:T(8,128)S(1)} custom-call(bf16[2048,320]{1,0:T(8,128)(2,1)S(1)} %get-tuple-element.24.modes, bf16[320,1024]{1,0:T(8,128)(2,1)S(1)} %get-tuple-element.25.own, bf16[320,1024]{1,0:T(8,128)(2,1)S(1)} %collective-permute-done.13.got, f32[2048,2048]{1,0:T(8,128)S(1)} %shard_map.48.refs_0_), custom_call_target="tpu_custom_call", output_to_operand_aliasing={{}: (3, {})} | custom-call | flops 2684354560 | bytes 8388608 | tf_op jit(solution)/shard_map/pallas_call | solution.py:229
  49.4 3.0 %shard_map.50 = (bf16[2048,2048]{1,0:T(8,128)(2,1)}, bf16[1792,1024]{1,0:T(8,128)(2,1)S(1)}) custom-call(bf16[2048,512]{1,0:T(8,128)(2,1)S(1)} %copy-done, bf16[512,1024]{1,0:T(8,128)(2,1)S(1)} %shard_map.47.piece, f32[2048,2048]{1,0:T(8,128)S(1)} %shard_map.49.total), custom_call_target="tpu_custom_call" | custom-call | flops 2147483648 | bytes 8388608 | tf_op jit(solution)/shard_map/pallas_call | solution.py:305
  52.4 3.4 %shard_map.51 = bf16[2048,2048]{1,0:T(8,128)(2,1)} custom-call(bf16[2048,512]{1,0:T(8,128)(2,1)S(1)} %copy-done, bf16[512,1024]{1,0:T(8,128)(2,1)S(1)} %collective-permute-done.12.piece, f32[2048,2048]{1,0:T(8,128)S(1)} %shard_map.49.total, bf16[1792,1024]{1,0:T(8,128)(2,1)S(1)} %get-tuple-element.27.rest, ...), custom_call_target="tpu_custom_call", output_to_operand_aliasing={{}: (4, {})} | custom-call | flops 2147483648 | bytes 8388608 | tf_op jit(solution)/shard_map/pallas_call | solution.py:305
  (13 shorter events, 0.1 us)
Async XLA Ops:
  0.0 16.6 %all-to-all-start = ((bf16[8,256,128]{2,1,0:T(8,128)(2,1)}), bf16[8,256,128]{2,1,0:T(8,128)(2,1)S(1)}, u32[]{:S(2)}, u32[]{:S(2)}) async-start(bf16[8,256,128]{2,1,0:T(8,128)(2,1)} %bitcast.1), calls=%async_computation | async-start | bytes 1048576 | tf_op jit(solution)/shard_map/all_to_all | solution.py:324
  6.4 1.9 %collective-permute-start = (s32[1,128]{1,0:T(1,128)}, s32[1,128]{1,0:T(1,128)S(1)}, u32[]{:S(2)}, u32[]{:S(2)}) collective-permute-start(s32[1,128]{1,0:T(1,128)} %mine_hbm.1), channel_id=1, source_target_pairs={{0,1},{1,0},{2,3},{3,2},{4,5},{5,4},{6,7},{7,6},{8,9},{9,8},{10,11... | collective-permute-start | bytes 1544 | tf_op jit(solution)/shard_map/ppermute | solution.py:54
  17.0 4.8 %collective-permute-start.4 = (bf16[32,1024]{1,0:T(8,128)(2,1)S(1)}, bf16[32,1024]{1,0:T(8,128)(2,1)S(1)}, u32[]{:S(2)}, u32[]{:S(2)}) collective-permute-start(bf16[32,1024]{1,0:T(8,128)(2,1)S(1)} %slice.17), channel_id=1, source_target_pairs={{0,16},{1,17},{2,18},{3,19},{4,20},{5,21},{6,22},{7,23},{8,24},{9,... | collective-permute-start | bytes 196616 | tf_op jit(solution)/shard_map/ppermute | solution.py:54
  18.3 7.9 %collective-permute-start.3 = (bf16[64,1024]{1,0:T(8,128)(2,1)S(1)}, bf16[64,1024]{1,0:T(8,128)(2,1)S(1)}, u32[]{:S(2)}, u32[]{:S(2)}) collective-permute-start(bf16[64,1024]{1,0:T(8,128)(2,1)S(1)} %get-tuple-element.29), channel_id=1, source_target_pairs={{0,4},{1,5},{2,6},{3,7},{4,0},{5,1},{6,2},{7,3},{8,12},{9,13},{10,... | collective-permute-start | bytes 393224 | tf_op jit(solution)/shard_map/ppermute | solution.py:54
  18.8 7.4 %collective-permute-start.1 = (bf16[64,1024]{1,0:T(8,128)(2,1)S(1)}, bf16[64,1024]{1,0:T(8,128)(2,1)S(1)}, u32[]{:S(2)}, u32[]{:S(2)}) collective-permute-start(bf16[64,1024]{1,0:T(8,128)(2,1)S(1)} %get-tuple-element.30), channel_id=1, source_target_pairs={{0,2},{1,3},{2,0},{3,1},{4,6},{5,7},{6,4},{7,5},{8,10},{9,11},{10,... | collective-permute-start | bytes 393224 | tf_op jit(solution)/shard_map/ppermute | solution.py:54
  18.8 8.5 %collective-permute-start.2 = (bf16[64,1024]{1,0:T(8,128)(2,1)S(1)}, bf16[64,1024]{1,0:T(8,128)(2,1)S(1)}, u32[]{:S(2)}, u32[]{:S(2)}) collective-permute-start(bf16[64,1024]{1,0:T(8,128)(2,1)S(1)} %get-tuple-element.30), channel_id=1, source_target_pairs={{0,6},{1,7},{2,4},{3,5},{4,2},{5,3},{6,0},{7,1},{8,14},{9,15},{10,... | collective-permute-start | bytes 393224 | tf_op jit(solution)/shard_map/ppermute | solution.py:54
  21.6 5.7 %collective-permute-start.5 = (bf16[64,1024]{1,0:T(8,128)(2,1)S(1)}, bf16[64,1024]{1,0:T(8,128)(2,1)S(1)}, u32[]{:S(2)}, u32[]{:S(2)}) collective-permute-start(bf16[64,1024]{1,0:T(8,128)(2,1)S(1)} %get-tuple-element.29), channel_id=1, source_target_pairs={{0,8},{1,9},{2,10},{3,11},{4,12},{5,13},{6,14},{7,15},{8,0},{9,1},... | collective-permute-start | bytes 393224 | tf_op jit(solution)/shard_map/ppermute | solution.py:54
  21.9 4.3 %collective-permute-start.6 = (bf16[32,1024]{1,0:T(8,128)(2,1)S(1)}, bf16[32,1024]{1,0:T(8,128)(2,1)S(1)}, u32[]{:S(2)}, u32[]{:S(2)}) collective-permute-start(bf16[32,1024]{1,0:T(8,128)(2,1)S(1)} %slice.17), channel_id=1, source_target_pairs={{0,24},{1,25},{2,26},{3,27},{4,28},{5,29},{6,30},{7,31},{8,16},{9,... | collective-permute-start | bytes 196616 | tf_op jit(solution)/shard_map/ppermute | solution.py:54
  27.4 10.8 %collective-permute-start.7 = (bf16[160,1024]{1,0:T(8,128)(2,1)S(1)}, bf16[160,1024]{1,0:T(8,128)(2,1)S(1)}, u32[]{:S(2)}, u32[]{:S(2)}) collective-permute-start(bf16[160,1024]{1,0:T(8,128)(2,1)S(1)} %get-tuple-element.21), channel_id=1, source_target_pairs={{0,2},{1,3},{2,0},{3,1},{4,6},{5,7},{6,4},{7,5},{8,10},{9,11},{10,... | collective-permute-start | bytes 983048 | tf_op jit(solution)/shard_map/ppermute | solution.py:54
  27.5 10.7 %collective-permute-start.8 = (bf16[160,1024]{1,0:T(8,128)(2,1)S(1)}, bf16[160,1024]{1,0:T(8,128)(2,1)S(1)}, u32[]{:S(2)}, u32[]{:S(2)}) collective-permute-start(bf16[160,1024]{1,0:T(8,128)(2,1)S(1)} %get-tuple-element.22), channel_id=1, source_target_pairs={{0,6},{1,7},{2,4},{3,5},{4,2},{5,3},{6,0},{7,1},{8,14},{9,15},{10,... | collective-permute-start | bytes 983048 | tf_op jit(solution)/shard_map/ppermute | solution.py:54
  28.5 9.7 %collective-permute-start.10 = (bf16[96,1024]{1,0:T(8,128)(2,1)S(1)}, bf16[96,1024]{1,0:T(8,128)(2,1)S(1)}, u32[]{:S(2)}, u32[]{:S(2)}) collective-permute-start(bf16[96,1024]{1,0:T(8,128)(2,1)S(1)} %get-tuple-element.23), channel_id=1, source_target_pairs={{0,16},{1,17},{2,18},{3,19},{4,20},{5,21},{6,22},{7,23},{8,24},{9,... | collective-permute-start | bytes 589832 | tf_op jit(solution)/shard_map/ppermute | solution.py:54
  28.7 9.4 %collective-permute-start.9 = (bf16[64,1024]{1,0:T(8,128)(2,1)S(1)}, bf16[64,1024]{1,0:T(8,128)(2,1)S(1)}, u32[]{:S(2)}, u32[]{:S(2)}) collective-permute-start(bf16[64,1024]{1,0:T(8,128)(2,1)S(1)} %collective-permute-done.3.refs_2_), channel_id=1, source_target_pairs={{0,8},{1,9},{2,10},{3,11},{4,12},{5,13},{6,14},{7,15},{8,0},{9,1},... | collective-permute-start | bytes 393224 | tf_op jit(solution)/shard_map/ppermute | solution.py:54
  29.6 4.7 %collective-permute-start.11 = (bf16[32,1024]{1,0:T(8,128)(2,1)S(1)}, bf16[32,1024]{1,0:T(8,128)(2,1)S(1)}, u32[]{:S(2)}, u32[]{:S(2)}) collective-permute-start(bf16[32,1024]{1,0:T(8,128)(2,1)S(1)} %slice.19), channel_id=1, source_target_pairs={{0,24},{1,25},{2,26},{3,27},{4,28},{5,29},{6,30},{7,31},{8,16},{9,... | collective-permute-start | bytes 196616 | tf_op jit(solution)/shard_map/ppermute | solution.py:54
  34.3 10.1 %collective-permute-start.13 = (bf16[320,1024]{1,0:T(8,128)(2,1)S(1)}, bf16[320,1024]{1,0:T(8,128)(2,1)S(1)}, u32[]{:S(2)}, u32[]{:S(2)}) collective-permute-start(bf16[320,1024]{1,0:T(8,128)(2,1)S(1)} %get-tuple-element.25.own), channel_id=1, source_target_pairs={{0,1},{1,0},{2,3},{3,2},{4,5},{5,4},{6,7},{7,6},{8,9},{9,8},{10,11... | collective-permute-start | bytes 1966088 | tf_op jit(solution)/shard_map/ppermute | solution.py:54
  38.3 14.1 %collective-permute-start.12 = (bf16[512,1024]{1,0:T(8,128)(2,1)S(1)}, bf16[512,1024]{1,0:T(8,128)(2,1)S(1)}, u32[]{:S(2)}, u32[]{:S(2)}) collective-permute-start(bf16[512,1024]{1,0:T(8,128)(2,1)S(1)} %shard_map.47.piece), channel_id=1, source_target_pairs={{0,1},{1,0},{2,3},{3,2},{4,5},{5,4},{6,7},{7,6},{8,9},{9,8},{10,11... | collective-permute-start | bytes 3145736 | tf_op jit(solution)/shard_map/ppermute | solution.py:54
  39.1 2.9 %collective-permute-start.14 = (bf16[208,1024]{1,0:T(8,128)(2,1)S(1)}, bf16[208,1024]{1,0:T(8,128)(2,1)S(1)}, u32[]{:S(2)}, u32[]{:S(2)}) collective-permute-start(bf16[208,1024]{1,0:T(8,128)(2,1)S(1)} %get-tuple-element.26), channel_id=1, source_target_pairs={{0,1},{1,0},{2,3},{3,2},{4,5},{5,4},{6,7},{7,6},{8,9},{9,8},{10,11... | collective-permute-start | bytes 1277960 | tf_op jit(solution)/shard_map/ppermute | solution.py:54
  44.3 5.1 %copy-start = (bf16[2048,512]{1,0:T(8,128)(2,1)S(1)}, bf16[2048,512]{1,0:T(8,128)(2,1)}, u32[]{:S(2)}) copy-start(bf16[2048,512]{1,0:T(8,128)(2,1)} %get-tuple-element.17.modes) | copy-start | bytes 6291460
